TPU v7x, 512 devices: a whole 4x8x8 slice. The times are simulated.
512 devices in a mesh: chan: 32 (over y, x), facet: 16 (over z, core).
Axes of the slice: x: 4, y: 8, z: 8, core: 2. Of those that a mesh axis runs over, the one named last changes fastest.
Arguments:
- start_image: float32 [64, 8192], P(None, 'facet'), may hold values from 0 to 3
- visibilities: bfloat16 [512, 64, 16, 256], P(('chan', 'facet')), may hold values from -12 to 12
- strip_index: int32 [512, 64, 16, 2], P(('chan', 'facet')), may hold values from 0 to 4095
- live_counts: int32 [512, 64, 16], P(('chan', 'facet')), may hold values from 0 to 128
- uv_kernels: bfloat16 [64, 16, 256, 256], P('chan', 'facet'), may hold values from -0.375 to 0.375
Outputs:
- final_image: float32 [64, 8192], P(None, 'facet')
Inputs may be any that keep to these rules, and one draw needn't show every extreme that they name: `strip_index`: each visibility block reads 2 image strips. The first live_counts of a block's 128 visibilities are live, the others are flagged.
All inputs are finite; a program needn't handle non-finite values.
Results may differ from a plain program's by a relative error of at most 0.0026.
Values may be sent and summed in bfloat16 or wider, within the bound.
A program may use at most 64 MiB of HBM per device.

v0:
```python
import jax
import jax.numpy as jnp
from jax import lax
from jax.sharding import PartitionSpec as P

STRIP = 128
VISB = 128
TERMS = 2
ITERS = 2


shrinkage = 0.05


def on_device(start_image, visibilities, strip_index, live_counts, uv_kernels):
    observed, picked_ids, live_now = (
        lax.all_to_all(
            lax.all_to_all(visibilities, "chan", split_axis=1, concat_axis=0, tiled=True),
            "facet",
            split_axis=2,
            concat_axis=0,
            tiled=True,
        ),
        lax.all_to_all(
            lax.all_to_all(strip_index, "chan", split_axis=1, concat_axis=0, tiled=True),
            "facet",
            split_axis=2,
            concat_axis=0,
            tiled=True,
        ),
        lax.all_to_all(
            lax.all_to_all(live_counts, "chan", split_axis=1, concat_axis=0, tiled=True),
            "facet",
            split_axis=2,
            concat_axis=0,
            tiled=True,
        ),
    )
    chan_count = lax.axis_size("chan")
    facet_count = lax.axis_size("facet")
    slot_count = observed.shape[0]
    chan_local = uv_kernels.shape[0]
    uv_local = uv_kernels.shape[1]
    all_channels = chan_local * chan_count
    all_uvtiles = uv_local * facet_count
    slab_rows = start_image.shape[0]
    facet_width = start_image.shape[1]
    full_width = facet_width * facet_count
    strip_count = slab_rows * full_width // STRIP
    step_size = strip_count / (2.5 * slot_count * all_channels * all_uvtiles)
    lane_ids = jnp.arange(2 * VISB, dtype=jnp.int32) % VISB
    live_mask = lane_ids < live_now[..., None]
    flat_ids = picked_ids.reshape(-1)
    estimate = start_image
    for iteration in range(ITERS):
        full_sky = lax.all_gather(estimate.astype(jnp.bfloat16), "facet", axis=1, tiled=True)
        sky_strips = full_sky.reshape(strip_count, STRIP)
        gathered = sky_strips[picked_ids].reshape(slot_count, chan_local, uv_local, TERMS * STRIP)
        predicted = jnp.einsum(
            "scup,cupq->scuq", gathered, uv_kernels, preferred_element_type=jnp.float32
        )
        residual = jnp.where(live_mask, predicted - observed.astype(jnp.float32), 0.0).astype(
            jnp.bfloat16
        )
        adjoint = jnp.einsum(
            "scuq,cupq->scup", residual, uv_kernels, preferred_element_type=jnp.float32
        )
        gradient = (
            jnp.zeros((strip_count, STRIP), jnp.float32)
            .at[flat_ids]
            .add(adjoint.reshape(-1, STRIP))
        )
        gradient = gradient.reshape(slab_rows, full_width)
        summed = lax.psum(gradient, ("chan", "facet"))
        facet_sum = lax.dynamic_slice_in_dim(
            summed, lax.axis_index("facet") * facet_width, facet_width, 1
        )
        descent = estimate - step_size * facet_sum
        estimate = jnp.maximum(descent - shrinkage, 0.0)
    return estimate


def solution(mesh):
    placed = (
        P(None, "facet"),
        P(("chan", "facet"), None, None, None),
        P(("chan", "facet"), None, None, None),
        P(("chan", "facet"), None, None),
        P("chan", "facet", None, None),
    )
    return jax.shard_map(
        on_device, mesh=mesh, in_specs=placed, out_specs=P(None, "facet"), check_vma=False
    )
```

profile of v0, /device:TPU:1, one launch (start us, length us, event | category | flops | bytes accessed | tf_op | source)
XLA Modules:
  0.0 772.4 jit_solution(1975982674927763844)
XLA Ops:
  6.5 1.4 copy.51
  8.0 10.5 %all-to-all-start.2 = ((s32[1,64,16]{2,0,1:T(1,128)}), s32[1,64,16]{2,0,1:T(1,128)S(1)}, u32[]{:S(2)}, u32[]{:S(2)}) async-start(s32[1,64,16]{2,0,1:T(1,128)} %copy.51), calls=%async_computation.2 | async-start | bytes 65536 | tf_op jit(solution)/shard_map/all_to_all | solution.py:32
  18.5 1.4 copy.47
  19.9 7.3 all-to-all-done.2
  27.2 3.9 all-to-all-start
  31.0 0.7 copy.52
  31.7 8.2 %all-to-all-done = s32[1,64,16,2]{2,3,0,1:T(2,128)S(1)} async-done(((s32[1,64,16,2]{2,3,0,1:T(2,128)}), s32[1,64,16,2]{2,3,0,1:T(2,128)S(1)}, u32[]{:S(2)}, u32[]{:S(2)}) %all-to-all-start) | async-done | bytes 8224 | tf_op jit(solution)/shard_map/all_to_all | solution.py:25
  39.9 13.6 %all-to-all-start.3 = ((s32[32,2,16]{0,1,2:T(2,128)}), s32[32,2,16]{0,1,2:T(2,128)S(1)}, u32[]{:S(2)}, u32[]{:S(2)}) async-start(s32[32,2,16]{0,1,2:T(2,128)} %copy.52), calls=%async_computation.3 | async-start | bytes 32768 | tf_op jit(solution)/shard_map/all_to_all | solution.py:31
  53.5 0.1 copy.49
  53.6 0.1 reshape.215
  53.7 7.1 all-to-all-done.3
  60.8 9.8 %all_to_all.78 = s32[16,1,128]{2,1,0:T(1,128)S(1)} all-to-all(s32[16,1,128]{2,1,0:T(1,128)S(1)} %reshape.215), channel_id=1, replica_groups=mesh['chan'=32,'facet'=16] {'facet'}, dimensions={0} | all-to-all | bytes 16384 | tf_op jit(solution)/shard_map/all_to_all | solution.py:24
  70.7 3.9 all-to-all-start.4
  74.6 1.5 convert_element_type.33
  76.3 0.5 broadcast.137
  76.8 0.7 reduce
  77.6 13.6 %all-to-all-done.4 = bf16[1,64,16,256]{3,2,0,1:T(8,128)(2,1)S(1)} async-done(((bf16[1,64,16,256]{3,2,0,1:T(8,128)(2,1)}), bf16[1,64,16,256]{3,2,0,1:T(8,128)(2,1)S(1)}, u32[]{:S(2)}, u32[]{:S(2)}) %all-to-all-start.4) | async-done | bytes 524320 | tf_op jit(solution)/shard_map/all_to_all | solution.py:18
  91.2 1.1 copy.58
  92.3 5.5 all-to-all-start.5
  97.8 0.3 copy.50
  98.2 0.6 reshape.159
  98.9 0.3 copy.55
  99.2 0.6 reshape.175
  99.8 19.2 %all-gather.3.cloned.1.call-done = bf16[64,8192]{1,0:T(8,128)(2,1)} async-done(((bf16[64,512]{1,0:T(8,128)(2,1)}), bf16[64,8192]{1,0:T(8,128)(2,1)}) %all-gather.3.cloned.1.call-update) | async-done | bytes 1048592 | tf_op jit(solution)/shard_map/all_gather | solution.py:56
  119.0 1.6 reshape.160
  120.6 6.2 gather_fusion
  126.8 0.3 reshape.161
  127.1 0.1 convert_bitcast_fusion
  127.2 0.1 copy.59
  127.4 0.4 convolution_bitcast_fusion.2
  127.8 0.8 copy.60
  128.6 1.8 reshape.193
  130.4 12.3 %scatter_custom_fusion = f32[4096,128]{1,0:T(8,128)S(1)} fusion(s32[2048]{0:T(1024)S(1)} %bitcast.104, f32[2048,128]{1,0:T(8,128)} %reshape.193, f32[]{:T(128)} %constant.12.clone.1), kind=kCustom, calls=%fused_computation.19 | custom fusion | flops 262144 | bytes 2097664 | tf_op jit(solution)/shard_map/scatter-add | solution.py:71
  142.8 1.5 reshape.165
  144.4 277.5 %all-reduce.3.cloned.1.call-done = f32[64,8192]{1,0:T(8,128)} async-done(((f32[64,8192]{1,0:T(8,128)}), f32[64,8192]{1,0:T(8,128)}) %all-reduce.3.cloned.1.call-update) | async-done | bytes 2097168 | tf_op jit(solution)/shard_map/psum | solution.py:74
  421.9 1.6 fusion.24
  423.5 0.2 all-reduce.5.cloned.1.call-start
  423.7 39.2 %all-gather.5.cloned.1.call-done = bf16[64,8192]{1,0:T(8,128)(2,1)} async-done(((bf16[64,512]{1,0:T(8,128)(2,1)}), bf16[64,8192]{1,0:T(8,128)(2,1)}) %all-gather.5.cloned.1.call-update) | async-done | bytes 1048592 | tf_op jit(solution)/shard_map/all_gather | solution.py:56
  463.0 1.6 reshape.166
  464.5 6.2 gather_fusion.1
  470.7 0.3 reshape.167
  471.1 0.5 convolution_bitcast_fusion
  471.5 0.8 copy.62
  472.3 0.8 reshape.201
  473.2 12.1 %scatter_custom_fusion.1 = f32[4096,128]{1,0:T(8,128)S(1)} fusion(s32[2048]{0:T(1024)} %bitcast.105, f32[2048,128]{1,0:T(8,128)S(1)} %reshape.201, f32[]{:T(128)} %constant.12.clone.1), kind=kCustom, calls=%fused_computation.17 | custom fusion | flops 262144 | bytes 2097664 | tf_op jit(solution)/shard_map/scatter-add | solution.py:71
  485.3 1.5 reshape.170
  486.8 277.4 %all-reduce.5.cloned.1.call-done = f32[64,8192]{1,0:T(8,128)} async-done(((f32[64,8192]{1,0:T(8,128)}), f32[64,8192]{1,0:T(8,128)}) %all-reduce.5.cloned.1.call-update) | async-done | bytes 2097168 | tf_op jit(solution)/shard_map/psum | solution.py:74
  764.2 1.7 add_maximum_fusion
  (24 shorter events, 0.5 us)
Async XLA Ops:
  6.5 120.8 %copy-start = (bf16[2,1,256,256]{3,2,1,0:T(8,128)(2,1)S(1)}, bf16[2,1,256,256]{3,2,1,0:T(8,128)(2,1)}, u32[]{:S(2)}) copy-start(bf16[2,1,256,256]{3,2,1,0:T(8,128)(2,1)} %param.9) | copy-start | bytes 786436
  8.0 19.2 %all-to-all-start.2 = ((s32[1,64,16]{2,0,1:T(1,128)}), s32[1,64,16]{2,0,1:T(1,128)S(1)}, u32[]{:S(2)}, u32[]{:S(2)}) async-start(s32[1,64,16]{2,0,1:T(1,128)} %copy.51), calls=%async_computation.2 | async-start | bytes 65536 | tf_op jit(solution)/shard_map/all_to_all | solution.py:32
  27.2 12.7 %all-to-all-start = ((s32[1,64,16,2]{2,3,0,1:T(2,128)}), s32[1,64,16,2]{2,3,0,1:T(2,128)S(1)}, u32[]{:S(2)}, u32[]{:S(2)}) async-start(s32[1,64,16,2]{2,3,0,1:T(2,128)} %copy.47), calls=%async_computation | async-start | bytes 131072 | tf_op jit(solution)/shard_map/all_to_all | solution.py:25
  39.9 20.9 %all-to-all-start.3 = ((s32[32,2,16]{0,1,2:T(2,128)}), s32[32,2,16]{0,1,2:T(2,128)S(1)}, u32[]{:S(2)}, u32[]{:S(2)}) async-start(s32[32,2,16]{0,1,2:T(2,128)} %copy.52), calls=%async_computation.3 | async-start | bytes 32768 | tf_op jit(solution)/shard_map/all_to_all | solution.py:31
  70.7 20.5 %all-to-all-start.4 = ((bf16[1,64,16,256]{3,2,0,1:T(8,128)(2,1)}), bf16[1,64,16,256]{3,2,0,1:T(8,128)(2,1)S(1)}, u32[]{:S(2)}, u32[]{:S(2)}) async-start(bf16[1,64,16,256]{3,2,0,1:T(8,128)(2,1)} %bitcast.99), calls=%async_computation.4 | async-start | bytes 1048576 | tf_op jit(solution)/shard_map/all_to_all | solution.py:18
  74.6 44.4 %all-gather.3.cloned.1.call-start = ((), (), s32[]{:S(2)}) async-start(), calls=%async_computation.6 | async-start | bytes 1114112 | tf_op jit(solution)/shard_map/all_gather | solution.py:56
  92.3 34.8 %all-to-all-start.5 = ((bf16[32,2,16,256]{3,0,1,2:T(8,128)(2,1)}), bf16[32,2,16,256]{3,0,1,2:T(8,128)(2,1)S(1)}, u32[]{:S(2)}, u32[]{:S(2)}) async-start(bf16[32,2,16,256]{3,0,1,2:T(8,128)(2,1)} %copy.58), calls=%async_computation.5 | async-start | bytes 1048576 | tf_op jit(solution)/shard_map/all_to_all | solution.py:17
  97.8 324.1 %all-reduce.3.cloned.1.call-start = ((), (), s32[]{:S(2)}) async-start(), calls=%async_computation.7 | async-start | bytes 4194304 | tf_op jit(solution)/shard_map/psum | solution.py:74
  99.8 30.6 %copy-start.2 = (s32[2048,1]{0,1:T(1,128)}, s32[2048,1]{0,1:T(1,128)S(1)}, u32[]{:S(2)}) copy-start(s32[2048,1]{0,1:T(1,128)S(1)} %compare_select_fusion.2) | copy-start | bytes 24580
  144.3 277.6 %copy-start.1 = (f32[64,512]{1,0:T(8,128)S(1)}, f32[64,512]{1,0:T(8,128)}, u32[]{:S(2)}) copy-start(f32[64,512]{1,0:T(8,128)} %param.5) | copy-start | bytes 393220
  144.3 318.6 %all-gather.5.cloned.1.call-start = ((), (), s32[]{:S(2)}) async-start(), calls=%async_computation.8 | async-start | bytes 1114112 | tf_op jit(solution)/shard_map/all_gather | solution.py:56
  423.5 340.7 %all-reduce.5.cloned.1.call-start = ((), (), s32[]{:S(2)}) async-start(), calls=%async_computation.9 | async-start | bytes 4194304 | tf_op jit(solution)/shard_map/psum | solution.py:74
Sparse Core Ops, SparseCore 0:
  77.5 41.4 all-gather.2
  144.5 277.3 all-reduce.2
  424.3 38.6 all-gather.4
  487.0 277.2 all-reduce.4
where the time goes:
time: 773 us; the launch traced here: 772 us
  waiting for transfers between devices  650 us (84%)
  starting transfers between devices  37.6 us (5%)
  local copies, waits for them, and re-layouts  31.1 us (4%)
  other arithmetic  30 us (4%)
  between operations  13.4 us (2%)
  blocking collectives  9.83 us (1%)
    psum x2, waiting for transfers between devices, on_device(): summed = lax.psum(gradient, ('chan', 'facet'))  555 us
    all_gather x2, waiting for transfers between devices, on_device(): lax.all_gather(estimate.astype(jnp.bfloat16), 'facet', axis=1, tiled=True)  58.4 us
    scatter-add x2, other arithmetic, on_device(): gradient = jnp.zeros((strip_count, STRIP), jnp.float32).at[flat_ids].add(...  24.4 us
  transfers between devices with their start and end apart: 9, of which 8 were waited for; matrix products, arithmetic and copies ran while one was open for 2% of the time, Pallas kernels for 0%

commit v1 on v0

v1 whole, which is shorter than its diff:
```python
import jax
import jax.numpy as jnp
from jax import lax
from jax.experimental import pallas as pl
from jax.experimental.pallas import tpu as pltpu
from jax.sharding import PartitionSpec as P

STRIP = 128
VISB = 128
TERMS = 2
ITERS = 2
NX = 4
NY = 8
NZ = 8
PLANE = NY * NZ
OWNERS = 2 * NX * PLANE
PIECE = 8

shrinkage = 0.05
MESH = pl.DeviceIdType.MESH


def reduce_kernel(
    final, step_size, g_ref, est_ref, out_ref, est_out, got1, sum1, got2, sum2, got3, sky, sems1, sems2, sems3, sems4, sems5, sems6
):
    chan = lax.axis_index("chan")
    facet = lax.axis_index("facet")
    y, x = chan // NX, chan % NX
    z, core = facet // 2, facet % 2
    spot = y * NZ + z

    partner = (chan, z * 2 + (1 - core))

    def on_x(dx):
        return (y * NX + lax.rem(x + dx, NX), facet)

    def on_plane(k):
        yy = lax.rem(y + k // NZ, NY)
        zz = lax.rem(z + k % NZ, NZ)
        return yy * NZ + zz, (yy * NX + x, zz * 2 + core)

    def on_chan(k):
        yy = lax.rem(y + k // NX, NY)
        xx = lax.rem(x + k % NX, NX)
        return (yy * NX + xx, facet)

    def copy(src, dst, send, recv, target):
        return pltpu.make_async_remote_copy(
            src_ref=src, dst_ref=dst, send_sem=send, recv_sem=recv, device_id=target, device_id_type=MESH
        )

    barrier = pltpu.get_barrier_semaphore()
    pl.semaphore_signal(barrier, inc=1, device_id=partner, device_id_type=MESH)
    for dx in range(1, NX):
        pl.semaphore_signal(barrier, inc=1, device_id=on_x(dx), device_id_type=MESH)

    @pl.loop(1, PLANE)
    def _(k):
        pl.semaphore_signal(barrier, inc=1, device_id=on_plane(k)[1], device_id_type=MESH)

    greeted = 1 + (NX - 1) + (PLANE - 1)
    if final:

        @pl.loop(1, NY)
        def _(dy):
            for dx in range(1, NX):
                pl.semaphore_signal(barrier, inc=1, device_id=on_chan(dy * NX + dx), device_id_type=MESH)

        greeted += (NY - 1) * (NX - 1)
    pl.semaphore_wait(barrier, greeted)

    order = [1, 3, 2, 0]

    def own_block(xx):
        return pl.ds((core * NX + xx) * PLANE, PLANE)

    def pair_copy(dx):
        xx = lax.rem(x + dx, NX)
        return copy(
            g_ref.at[pl.ds(((1 - core) * NX + xx) * PLANE, PLANE)],
            got1.at[dx],
            sems1.at[0, dx],
            sems1.at[1, dx],
            partner,
        )

    for dx in order:
        pair_copy(dx).start()

    def x_copy(dx):
        return copy(sum1.at[dx], got2.at[dx], sems2.at[0, dx], sems2.at[1, dx], on_x(dx))

    for dx in order[:-1]:
        pair_copy(dx).wait_recv()
        base = (core * NX + lax.rem(x + dx, NX)) * PLANE

        @pl.loop(0, PLANE // 8)
        def _(i):
            total = g_ref[pl.ds(base + i * 8, 8)].astype(jnp.float32) + got1[dx, pl.ds(i * 8, 8)].astype(jnp.float32)
            sum1[dx, pl.ds(i * 8, 8)] = total.astype(jnp.bfloat16)

        x_copy(dx).start()
    pair_copy(0).wait_recv()
    for dx in order[:-1]:
        x_copy(dx).wait_recv()
    base = (core * NX + x) * PLANE

    @pl.loop(0, PLANE // 8)
    def _(i):
        rows = pl.ds(i * 8, 8)
        total = g_ref[pl.ds(base + i * 8, 8)].astype(jnp.float32) + got1[0, rows].astype(jnp.float32)
        for dx in order[:-1]:
            total += got2[dx, rows].astype(jnp.float32)
        sum2[rows] = total.astype(jnp.bfloat16)

    def plane_copy(k):
        place, target = on_plane(k)
        return copy(sum2.at[place], got3.at[k], sems3.at[0, k], sems3.at[1, k], target)

    @pl.loop(1, PLANE)
    def _(k):
        plane_copy(k).start()

    @pl.loop(1, PLANE)
    def _(k):
        plane_copy(k).wait_recv()

    gradient = sum2[spot].astype(jnp.float32)
    for k in range(1, PLANE):
        gradient += got3[k].astype(jnp.float32)
    estimate = jnp.maximum(est_ref[...] - step_size * gradient - shrinkage, 0.0)

    if final:
        sky[chan] = estimate

        def chan_copy(k):
            return copy(sky.at[chan], sky.at[chan], sems4.at[0, k], sems4.at[1, k], on_chan(k))

        @pl.loop(1, NY * NX)
        def _(k):
            chan_copy(k).start()

        @pl.loop(1, NY * NX)
        def _(k):
            chan_copy(k).wait()

        out_ref[...] = sky[...]
        est_out[...] = estimate
    else:
        est_out[...] = estimate
        mine = (core * NX + x) * PLANE + spot
        sky[mine] = estimate.astype(jnp.bfloat16)

        def spread_plane(k):
            return copy(sky.at[mine], sky.at[mine], sems4.at[0, k], sems4.at[1, k], on_plane(k)[1])

        @pl.loop(1, PLANE)
        def _(k):
            spread_plane(k).start()

        @pl.loop(1, PLANE)
        def _(k):
            spread_plane(k).wait_recv()

        def spread_x(dx):
            block = sky.at[own_block(x)]
            return copy(block, block, sems5.at[0, dx], sems5.at[1, dx], on_x(dx))

        def spread_pair(dx):
            block = sky.at[own_block(lax.rem(x + dx, NX))]
            return copy(block, block, sems6.at[0, dx], sems6.at[1, dx], partner)

        for dx in order[:-1]:
            spread_x(dx).start()
        spread_pair(0).start()
        for dx in order[:-1]:
            spread_x(dx).wait_recv()
            spread_pair(NX - dx).start()
        for dx in range(NX):
            spread_pair(dx).wait()
        for dx in order[:-1]:
            spread_x(dx).wait_send()

        @pl.loop(1, PLANE)
        def _(k):
            spread_plane(k).wait_send()

        out_ref[...] = sky[...]

    for dx in order:
        pair_copy(dx).wait_send()
    for dx in order[:-1]:
        x_copy(dx).wait_send()

    @pl.loop(1, PLANE)
    def _(k):
        plane_copy(k).wait_send()


def reduce_step(final, step_size, gradient, estimate):
    def body(*refs):
        reduce_kernel(final, step_size, *refs)

    dma = pltpu.SemaphoreType.DMA
    if final:
        out = jax.ShapeDtypeStruct((NY * NX, PIECE, STRIP), jnp.float32)
    else:
        out = jax.ShapeDtypeStruct((OWNERS, PIECE, STRIP), jnp.bfloat16)
    return pl.pallas_call(
        body,
        out_shape=(out, jax.ShapeDtypeStruct((PIECE, STRIP), jnp.float32)),
        in_specs=[pl.BlockSpec(memory_space=pltpu.VMEM)] * 2,
        out_specs=(pl.BlockSpec(memory_space=pltpu.VMEM),) * 2,
        scratch_shapes=[
            pltpu.VMEM((NX, PLANE, PIECE, STRIP), jnp.bfloat16),
            pltpu.VMEM((NX, PLANE, PIECE, STRIP), jnp.bfloat16),
            pltpu.VMEM((NX, PLANE, PIECE, STRIP), jnp.bfloat16),
            pltpu.VMEM((PLANE, PIECE, STRIP), jnp.bfloat16),
            pltpu.VMEM((PLANE, PIECE, STRIP), jnp.bfloat16),
            pltpu.VMEM(out.shape, out.dtype),
            dma((2, NX)),
            dma((2, NX)),
            dma((2, PLANE)),
            dma((2, PLANE)),
            dma((2, NX)),
            dma((2, NX)),
        ],
        compiler_params=pltpu.CompilerParams(collective_id=1 if final else 0, has_side_effects=True),
        name="reduce_final" if final else "reduce_sky",
    )(gradient, estimate)


def owner_order(strip):
    quarter = strip % 4
    core = strip // 4 % 2
    z = strip // 8 % 8
    low_row = strip // 64 % 2
    x = strip // 128 % 4
    y = strip // 512
    return (((core * NX + x) * NY + y) * NZ + z) * PIECE + low_row * 4 + quarter


def on_device(start_image, visibilities, strip_index, live_counts, uv_kernels):
    observed, picked_ids, live_now = (
        lax.all_to_all(
            lax.all_to_all(array, "chan", split_axis=1, concat_axis=0, tiled=True),
            "facet",
            split_axis=2,
            concat_axis=0,
            tiled=True,
        )
        for array in (visibilities, owner_order(strip_index), live_counts)
    )
    chan_count = lax.axis_size("chan")
    facet_count = lax.axis_size("facet")
    slot_count = observed.shape[0]
    chan_local = uv_kernels.shape[0]
    uv_local = uv_kernels.shape[1]
    all_channels = chan_local * chan_count
    all_uvtiles = uv_local * facet_count
    slab_rows = start_image.shape[0]
    facet_width = start_image.shape[1]
    strip_count = slab_rows * facet_width * facet_count // STRIP
    step_size = strip_count / (2.5 * slot_count * all_channels * all_uvtiles)
    lane_ids = jnp.arange(2 * VISB, dtype=jnp.int32) % VISB
    live_mask = lane_ids < live_now[..., None]
    flat_ids = picked_ids.reshape(-1)
    pieces = start_image.reshape(NY * NX, PIECE, STRIP)
    estimate = lax.dynamic_index_in_dim(pieces, lax.axis_index("chan"), 0, keepdims=False)
    sky = lax.all_gather(start_image.astype(jnp.bfloat16), "facet", axis=0, tiled=False)
    sky = sky.reshape(NZ, 2, NY, NX, 2, 4, STRIP).transpose(1, 3, 2, 0, 4, 5, 6)
    for iteration in range(ITERS):
        sky_strips = sky.reshape(strip_count, STRIP)
        gathered = sky_strips[picked_ids].reshape(slot_count, chan_local, uv_local, TERMS * STRIP)
        predicted = jnp.einsum(
            "scup,cupq->scuq", gathered, uv_kernels, preferred_element_type=jnp.float32
        )
        residual = jnp.where(live_mask, predicted - observed.astype(jnp.float32), 0.0).astype(
            jnp.bfloat16
        )
        adjoint = jnp.einsum(
            "scuq,cupq->scup", residual, uv_kernels, preferred_element_type=jnp.float32
        )
        gradient = (
            jnp.zeros((strip_count, STRIP), jnp.float32)
            .at[flat_ids]
            .add(adjoint.reshape(-1, STRIP))
        )
        gradient = gradient.astype(jnp.bfloat16).reshape(OWNERS, PIECE, STRIP)
        sky, estimate = reduce_step(iteration == ITERS - 1, step_size, gradient, estimate)
    return sky.reshape(slab_rows, facet_width)


def solution(mesh):
    placed = (
        P(None, "facet"),
        P(("chan", "facet"), None, None, None),
        P(("chan", "facet"), None, None, None),
        P(("chan", "facet"), None, None),
        P("chan", "facet", None, None),
    )
    return jax.shard_map(
        on_device, mesh=mesh, in_specs=placed, out_specs=P(None, "facet"), check_vma=False
    )
```

time: 773 us -> 262 us (0.34)
  waiting for transfers between devices: 650 us -> 53.6 us
  Pallas kernels: 0 us -> 86.2 us
    psum x2 -> x0, waiting for transfers between devices: 555 us -> none  [on_device(): summed = lax.psum(gradient, ('chan', 'facet'))]
    pallas_call x0 -> x2, Pallas kernels: none -> 86.2 us  [reduce_step(): pl.pallas_call(body, out_shape=(out, jax.ShapeDtypeStruct((PIECE, STRIP),...]
    all_gather x2 -> x1, waiting for transfers between devices: 58.4 us -> 19.1 us  [on_device(): lax.all_gather(start_image.astype(jnp.bfloat16), 'facet', axis=0, tiled=F...]
  transfers between devices with their start and end apart: 9 -> 6, of which waited for: 8 -> 5; matrix products, arithmetic and copies ran while one was open for 2% -> 7% of each run, Pallas kernels for 0% -> 0%
where the time goes in v1:
time: 262 us; the launch traced here: 261 us
  Pallas kernels  86.2 us (33%)
  waiting for transfers between devices  53.6 us (20%)
  starting transfers between devices  37.3 us (14%)
  other arithmetic  30.7 us (12%)
  local copies, waits for them, and re-layouts  29.1 us (11%)
  between operations  13.7 us (5%)
  blocking collectives  9.83 us (4%)
    pallas_call x2, Pallas kernels, reduce_step(): pl.pallas_call(body, out_shape=(out, jax.ShapeDtypeStruct((PIECE, STRIP),...  86.2 us
    all_to_all x3, waiting for transfers between devices, on_device(): lax.all_to_all(array, 'chan', split_axis=1, concat_axis=0, tiled=True)  27.3 us
    scatter-add x2, other arithmetic, on_device(): gradient = jnp.zeros((strip_count, STRIP), jnp.float32).at[flat_ids].add(...  24.5 us
    all_gather x1, waiting for transfers between devices, on_device(): lax.all_gather(start_image.astype(jnp.bfloat16), 'facet', axis=0, tiled=F...  19.1 us
    all_to_all x2, starting transfers between devices, on_device(): lax.all_to_all(lax.all_to_all(array, 'chan', split_axis=1, concat_axis=0,...  19.1 us
    all_to_all x3, starting transfers between devices, on_device(): lax.all_to_all(array, 'chan', split_axis=1, concat_axis=0, tiled=True)  18.3 us
    gather x2, local copies, waits for them, and re-layouts, on_device(): sky_strips[picked_ids]  13.1 us
    all_to_all x1, blocking collectives, on_device(): lax.all_to_all(lax.all_to_all(array, 'chan', split_axis=1, concat_axis=0,...  9.83 us
  transfers between devices with their start and end apart: 6, of which 5 were waited for; matrix products, arithmetic and copies ran while one was open for 7% of the time, Pallas kernels for 0%

profile of v1, /device:TPU:1, one launch (start us, length us, event | category | flops | bytes accessed | tf_op | source)
XLA Modules:
  0.0 261.3 jit_solution(10704035169499137852)
XLA Ops:
  6.5 1.4 copy.61
  8.0 10.5 %all-to-all-start.2 = ((s32[1,64,16]{2,0,1:T(1,128)}), s32[1,64,16]{2,0,1:T(1,128)S(1)}, u32[]{:S(2)}, u32[]{:S(2)}) async-start(s32[1,64,16]{2,0,1:T(1,128)} %copy.61), calls=%async_computation.2 | async-start | bytes 65536 | tf_op jit(solution)/shard_map/all_to_all | solution.py:246
  18.5 0.8 copy.54
  19.3 1.7 fusion.29
  21.0 6.2 %all-to-all-done.2 = s32[1,64,16]{2,0,1:T(1,128)S(1)} async-done(((s32[1,64,16]{2,0,1:T(1,128)}), s32[1,64,16]{2,0,1:T(1,128)S(1)}, u32[]{:S(2)}, u32[]{:S(2)}) %all-to-all-start.2) | async-done | bytes 4128 | tf_op jit(solution)/shard_map/all_to_all | solution.py:246
  27.2 3.9 %all-to-all-start = ((s32[1,64,16,2]{2,3,0,1:T(2,128)}), s32[1,64,16,2]{2,3,0,1:T(2,128)S(1)}, u32[]{:S(2)}, u32[]{:S(2)}) async-start(s32[1,64,16,2]{2,3,0,1:T(2,128)} %fusion.29), calls=%async_computation | async-start | bytes 131072 | tf_op jit(solution)/shard_map/all_to_all | solution.py:246
  31.0 0.7 copy.62
  31.7 8.2 %all-to-all-done = s32[1,64,16,2]{2,3,0,1:T(2,128)S(1)} async-done(((s32[1,64,16,2]{2,3,0,1:T(2,128)}), s32[1,64,16,2]{2,3,0,1:T(2,128)S(1)}, u32[]{:S(2)}, u32[]{:S(2)}) %all-to-all-start) | async-done | bytes 8224 | tf_op jit(solution)/shard_map/all_to_all | solution.py:246
  39.9 13.6 %all-to-all-start.3 = ((s32[32,2,16]{0,1,2:T(2,128)}), s32[32,2,16]{0,1,2:T(2,128)S(1)}, u32[]{:S(2)}, u32[]{:S(2)}) async-start(s32[32,2,16]{0,1,2:T(2,128)} %copy.62), calls=%async_computation.3 | async-start | bytes 32768 | tf_op jit(solution)/shard_map/all_to_all | solution.py:245
  53.5 0.1 copy.59
  53.6 0.1 reshape.229
  53.7 7.1 %all-to-all-done.3 = s32[32,2,16]{0,1,2:T(2,128)S(1)} async-done(((s32[32,2,16]{0,1,2:T(2,128)}), s32[32,2,16]{0,1,2:T(2,128)S(1)}, u32[]{:S(2)}, u32[]{:S(2)}) %all-to-all-start.3) | async-done | bytes 4128 | tf_op jit(solution)/shard_map/all_to_all | solution.py:245
  60.8 9.8 %all_to_all.78 = s32[16,1,128]{2,1,0:T(1,128)S(1)} all-to-all(s32[16,1,128]{2,1,0:T(1,128)S(1)} %reshape.229), channel_id=1, replica_groups=mesh['chan'=32,'facet'=16] {'facet'}, dimensions={0} | all-to-all | bytes 16384 | tf_op jit(solution)/shard_map/all_to_all | solution.py:245
  70.7 3.9 %all-to-all-start.4 = ((bf16[1,64,16,256]{3,2,0,1:T(8,128)(2,1)}), bf16[1,64,16,256]{3,2,0,1:T(8,128)(2,1)S(1)}, u32[]{:S(2)}, u32[]{:S(2)}) async-start(bf16[1,64,16,256]{3,2,0,1:T(8,128)(2,1)} %bitcast.111), calls=%async_computation.4 | async-start | bytes 1048576 | tf_op jit(solution)/shard_map/all_to_all | solution.py:246
  74.6 1.5 convert_element_type.36
  76.2 0.6 dynamic-slice_bitcast_fusion.refs_1_
  76.9 0.5 broadcast.156
  77.5 0.6 reduce
  78.1 0.1 reshape.230
  78.2 13.0 %all-to-all-done.4 = bf16[1,64,16,256]{3,2,0,1:T(8,128)(2,1)S(1)} async-done(((bf16[1,64,16,256]{3,2,0,1:T(8,128)(2,1)}), bf16[1,64,16,256]{3,2,0,1:T(8,128)(2,1)S(1)}, u32[]{:S(2)}, u32[]{:S(2)}) %all-to-all-start.4) | async-done | bytes 524320 | tf_op jit(solution)/shard_map/all_to_all | solution.py:246
  91.2 1.1 copy.69
  92.3 5.5 %all-to-all-start.5 = ((bf16[32,2,16,256]{3,0,1,2:T(8,128)(2,1)}), bf16[32,2,16,256]{3,0,1,2:T(8,128)(2,1)S(1)}, u32[]{:S(2)}, u32[]{:S(2)}) async-start(bf16[32,2,16,256]{3,0,1,2:T(8,128)(2,1)} %copy.69), calls=%async_computation.5 | async-start | bytes 1048576 | tf_op jit(solution)/shard_map/all_to_all | solution.py:245
  97.8 0.3 copy.60
  98.2 0.3 copy.66
  98.4 0.6 reshape.187
  99.1 0.7 reshape.168
  99.7 19.1 %all-gather.3.cloned.1.call-done = bf16[1024,512]{1,0:T(8,128)(2,1)} async-done(((bf16[64,512]{1,0:T(8,128)(2,1)}), bf16[1024,512]{1,0:T(8,128)(2,1)}) %all-gather.3.cloned.1.call-update) | async-done | bytes 1048592 | tf_op jit(solution)/shard_map/all_gather | solution.py:270
  118.9 1.3 reshape.169
  120.2 0.6 copy.64
  120.8 6.2 %gather_fusion = bf16[2048,128]{1,0:T(8,128)(2,1)S(1)} fusion(bf16[4096,128]{1,0:T(8,128)(2,1)S(1)} %bitcast.106, s32[2048]{0:T(1024)S(1)} %broadcast_clamp_fusion), kind=kCustom, calls=%fused_computation | custom fusion | bytes 1056768 | tf_op jit(solution)/shard_map/gather | solution.py:274
  127.0 0.3 reshape.171
  127.3 0.1 convert_bitcast_fusion
  127.4 0.1 copy.70
  127.6 0.4 convolution_bitcast_fusion.2
  128.0 0.8 copy.71
  128.8 1.8 reshape.205
  130.6 12.5 %scatter_custom_fusion = f32[4096,128]{1,0:T(8,128)S(1)} fusion(s32[2048]{0:T(1024)S(1)} %bitcast.116, f32[2048,128]{1,0:T(8,128)} %reshape.205, f32[]{:T(128)} %constant.113.clone.1), kind=kCustom, calls=%fused_computation.21 | custom fusion | flops 262144 | bytes 2097664 | tf_op jit(solution)/shard_map/scatter-add | solution.py:287
  143.2 1.1 convert_bitcast_fusion.2.refs_0_
  144.2 50.8 %reduce_sky.1 = (bf16[512,8,128]{2,1,0:T(8,128)(2,1)}, f32[8,128]{1,0:T(8,128)}) custom-call(bf16[512,8,128]{2,1,0:T(8,128)(2,1)} %convert_bitcast_fusion.2.refs_0_, f32[8,128]{1,0:T(8,128)} %dynamic-slice_bitcast_fusion.refs_1_), custom_call_target="tpu_custom_call" | custom-call | tf_op jit(solution)/shard_map/reduce_sky/pallas_call | solution.py:209
  195.1 7.0 %gather_fusion.1 = bf16[2048,128]{1,0:T(8,128)(2,1)S(1)} fusion(bf16[4096,128]{1,0:T(8,128)(2,1)} %bitcast.107, s32[2048]{0:T(1024)S(1)} %broadcast_clamp_fusion), kind=kCustom, calls=%fused_computation.1 | custom fusion | bytes 1056768 | tf_op jit(solution)/shard_map/gather | solution.py:274
  202.0 0.3 reshape.178
  202.4 0.4 convolution_bitcast_fusion
  202.8 0.8 copy.73
  203.7 0.8 reshape.213
  204.5 12.0 %scatter_custom_fusion.1 = f32[4096,128]{1,0:T(8,128)S(1)} fusion(s32[2048]{0:T(1024)S(1)} %bitcast.117, f32[2048,128]{1,0:T(8,128)S(1)} %reshape.213, f32[]{:T(128)} %constant.113.clone.1), kind=kCustom, calls=%fused_computation.19 | custom fusion | flops 262144 | bytes 2097156 | tf_op jit(solution)/shard_map/scatter-add | solution.py:287
  216.5 1.1 convert_bitcast_fusion.1.refs_0_
  217.6 35.3 %reduce_final.1 = (f32[32,8,128]{2,1,0:T(8,128)}, f32[8,128]{1,0:T(8,128)}) custom-call(bf16[512,8,128]{2,1,0:T(8,128)(2,1)} %convert_bitcast_fusion.1.refs_0_, f32[8,128]{1,0:T(8,128)} %get-tuple-element.9.refs_1_), custom_call_target="tpu_custom_call" | custom-call | tf_op jit(solution)/shard_map/reduce_final/pallas_call | solution.py:209
  252.9 1.6 reshape.182
  (17 shorter events, 0.3 us)
Async XLA Ops:
  6.5 121.0 %copy-start = (bf16[2,1,256,256]{3,2,1,0:T(8,128)(2,1)S(1)}, bf16[2,1,256,256]{3,2,1,0:T(8,128)(2,1)}, u32[]{:S(2)}) copy-start(bf16[2,1,256,256]{3,2,1,0:T(8,128)(2,1)} %param.9) | copy-start | bytes 786436
  6.5 69.7 %copy-start.1 = (f32[64,512]{1,0:T(8,128)S(1)}, f32[64,512]{1,0:T(8,128)}, u32[]{:S(2)}) copy-start(f32[64,512]{1,0:T(8,128)} %param.5) | copy-start | bytes 393220
  8.0 19.2 %all-to-all-start.2 = ((s32[1,64,16]{2,0,1:T(1,128)}), s32[1,64,16]{2,0,1:T(1,128)S(1)}, u32[]{:S(2)}, u32[]{:S(2)}) async-start(s32[1,64,16]{2,0,1:T(1,128)} %copy.61), calls=%async_computation.2 | async-start | bytes 65536 | tf_op jit(solution)/shard_map/all_to_all | solution.py:246
  27.2 12.8 %all-to-all-start = ((s32[1,64,16,2]{2,3,0,1:T(2,128)}), s32[1,64,16,2]{2,3,0,1:T(2,128)S(1)}, u32[]{:S(2)}, u32[]{:S(2)}) async-start(s32[1,64,16,2]{2,3,0,1:T(2,128)} %fusion.29), calls=%async_computation | async-start | bytes 131072 | tf_op jit(solution)/shard_map/all_to_all | solution.py:246
  39.9 20.9 %all-to-all-start.3 = ((s32[32,2,16]{0,1,2:T(2,128)}), s32[32,2,16]{0,1,2:T(2,128)S(1)}, u32[]{:S(2)}, u32[]{:S(2)}) async-start(s32[32,2,16]{0,1,2:T(2,128)} %copy.62), calls=%async_computation.3 | async-start | bytes 32768 | tf_op jit(solution)/shard_map/all_to_all | solution.py:245
  70.7 20.5 %all-to-all-start.4 = ((bf16[1,64,16,256]{3,2,0,1:T(8,128)(2,1)}), bf16[1,64,16,256]{3,2,0,1:T(8,128)(2,1)S(1)}, u32[]{:S(2)}, u32[]{:S(2)}) async-start(bf16[1,64,16,256]{3,2,0,1:T(8,128)(2,1)} %bitcast.111), calls=%async_computation.4 | async-start | bytes 1048576 | tf_op jit(solution)/shard_map/all_to_all | solution.py:246
  74.6 44.3 %all-gather.3.cloned.1.call-start = ((), (), s32[]{:S(2)}) async-start(), calls=%async_computation.6 | async-start | bytes 1114112 | tf_op jit(solution)/shard_map/all_gather | solution.py:270
  92.3 35.1 %all-to-all-start.5 = ((bf16[32,2,16,256]{3,0,1,2:T(8,128)(2,1)}), bf16[32,2,16,256]{3,0,1,2:T(8,128)(2,1)S(1)}, u32[]{:S(2)}, u32[]{:S(2)}) async-start(bf16[32,2,16,256]{3,0,1,2:T(8,128)(2,1)} %copy.69), calls=%async_computation.5 | async-start | bytes 1048576 | tf_op jit(solution)/shard_map/all_to_all | solution.py:245
Sparse Core Ops, SparseCore 0:
  77.5 41.2 all-gather.2

commit v2 on v1

--- a/solution.py
+++ b/solution.py
@@ -15,9 +15,221 @@
 PLANE = NY * NZ
 OWNERS = 2 * NX * PLANE
 PIECE = 8
+NEAR = 2 * NX
+
+FLAGGED = 1024.0
 
 shrinkage = 0.05
 MESH = pl.DeviceIdType.MESH
+
+
+def exchange_kernel(
+    start_ref,
+    meta_ref,
+    vis_ref,
+    sky_out,
+    index_out,
+    vis_out,
+    sky,
+    meta1,
+    packed,
+    index_in,
+    vis1,
+    vis_in,
+    sky_plane,
+    sky_x,
+    sky_pair,
+    meta_near,
+    meta_plane,
+    vis_near,
+    vis_plane,
+):
+    chan = lax.axis_index("chan")
+    facet = lax.axis_index("facet")
+    y, x = chan // NX, chan % NX
+    z, core = facet // 2, facet % 2
+    spot = y * NZ + z
+
+    def near(i):
+        cc = lax.rem(core + i // NX, 2)
+        xx = lax.rem(x + i % NX, NX)
+        return cc * NX + xx, (y * NX + xx, z * 2 + cc)
+
+    def on_plane(k):
+        yy = lax.rem(y + k // NZ, NY)
+        zz = lax.rem(z + k % NZ, NZ)
+        return yy * NZ + zz, (yy * NX + x, zz * 2 + core)
+
+    def copy(src, dst, sems, at, target):
+        return pltpu.make_async_remote_copy(
+            src_ref=src,
+            dst_ref=dst,
+            send_sem=sems.at[0, at],
+            recv_sem=sems.at[1, at],
+            device_id=target,
+            device_id_type=MESH,
+        )
+
+    barrier = pltpu.get_barrier_semaphore()
+    for i in range(1, NEAR):
+        pl.semaphore_signal(barrier, inc=1, device_id=near(i)[1], device_id_type=MESH)
+
+    @pl.loop(1, PLANE)
+    def _(k):
+        pl.semaphore_signal(barrier, inc=1, device_id=on_plane(k)[1], device_id_type=MESH)
+
+    pl.semaphore_wait(barrier, NEAR - 1 + PLANE - 1)
+
+    def spread_plane(k):
+        return copy(start_ref, sky.at[near(0)[0] * PLANE + spot], sky_plane, k, on_plane(k)[1])
+
+    def own_block(xx):
+        return sky.at[pl.ds((core * NX + xx) * PLANE, PLANE)]
+
+    def spread_x(dx):
+        return copy(own_block(x), own_block(x), sky_x, dx, near(dx)[1])
+
+    def spread_pair(dx):
+        block = own_block(lax.rem(x + dx, NX))
+        return copy(block, block, sky_pair, dx, near(NX)[1])
+
+    def near_meta(i):
+        return copy(meta_ref.at[near(i)[0]], meta1.at[i], meta_near, i, near(i)[1])
+
+    def near_vis(i):
+        block = vis_ref.at[pl.ds(near(i)[0] * PLANE, PLANE)]
+        return copy(block, vis1.at[pl.ds(i * PLANE, PLANE)], vis_near, i, near(i)[1])
+
+    def plane_meta(k):
+        place, target = on_plane(k)
+        return copy(packed.at[place], index_in.at[k], meta_plane, k, target)
+
+    @pl.loop(1, PLANE)
+    def _(k):
+        spread_plane(k).start()
+
+    for i in range(1, NEAR):
+        near_meta(i).start()
+    for i in range(1, NEAR):
+        near_vis(i).start()
+
+    def forward(i):
+        if i == 0:
+            base = near(0)[0] * PLANE
+            held = vis_ref
+        else:
+            base = i * PLANE
+            held = vis1
+        vis_in[0, i] = held[base + spot]
+
+        @pl.loop(1, PLANE)
+        def _(k):
+            place, target = on_plane(k)
+            copy(held.at[base + place], vis_in.at[k, i], vis_plane, 0, target).start()
+
+    for i in range(1, NEAR):
+        near_meta(i).wait_recv()
+    lane = lax.broadcasted_iota(jnp.int32, (32, STRIP), 1)
+    place = lax.broadcasted_iota(jnp.int32, (32, STRIP), 0)
+    belongs = lane // 4 == place
+    column = lax.broadcasted_iota(jnp.int32, (STRIP, STRIP), 1)
+    source = lax.broadcasted_iota(jnp.int32, (STRIP, STRIP), 0)
+    total = jnp.zeros((4 * 32, STRIP), jnp.float32)
+    for i in range(NEAR):
+        strips = meta_ref[near(0)[0]] if i == 0 else meta1[i]
+        high = jnp.floor(strips * (1.0 / 64.0))
+        low = strips - 64.0 * high
+        spread = jnp.concatenate(
+            [
+                jnp.where(belongs, jnp.broadcast_to(part[h : h + 1], (32, STRIP)), 0.0)
+                for part in (high, low)
+                for h in range(2)
+            ],
+            axis=0,
+        )
+        move = jnp.where(column == 4 * i + source % 4, 1.0, 0.0).astype(jnp.bfloat16)
+        total += jnp.dot(spread.astype(jnp.bfloat16), move, preferred_element_type=jnp.float32)
+    rows = 64.0 * total[:64] + total[64:]
+    for d in range(PLANE):
+        packed[d] = rows[d : d + 1]
+    index_in[0] = packed[spot]
+
+    @pl.loop(1, PLANE)
+    def _(k):
+        plane_meta(k).start()
+
+    sky[near(0)[0] * PLANE + spot] = start_ref[...]
+
+    @pl.loop(1, PLANE)
+    def _(k):
+        spread_plane(k).wait_recv()
+
+    for dx in range(1, NX):
+        spread_x(dx).start()
+    spread_pair(0).start()
+    forward(0)
+    for i in range(1, NEAR):
+        if i < NX:
+            spread_x(i).wait_recv()
+            spread_pair(NX - i).start()
+        near_vis(i).wait_recv()
+        forward(i)
+
+    @pl.loop(1, PLANE)
+    def _(k):
+        plane_meta(k).wait()
+
+    for dx in range(NX):
+        spread_pair(dx).wait()
+    sky_out[...] = sky[...]
+    index_out[...] = index_in[...]
+    arrived = vis_in.at[pl.ds(1, PLANE - 1)]
+    copy(arrived, arrived, vis_plane, 0, near(NX)[1]).wait()
+    vis_out[...] = vis_in[...]
+    for dx in range(1, NX):
+        spread_x(dx).wait_send()
+    for i in range(1, NEAR):
+        near_meta(i).wait_send()
+        near_vis(i).wait_send()
+
+    @pl.loop(1, PLANE)
+    def _(k):
+        spread_plane(k).wait_send()
+
+
+def exchange(start_piece, strips, visibilities):
+    dma = pltpu.SemaphoreType.DMA
+    vmem = pltpu.VMEM
+    sky = (OWNERS, PIECE, STRIP)
+    index = (PLANE, 1, STRIP)
+    blocks = (PLANE, NEAR, 4, STRIP)
+    return pl.pallas_call(
+        exchange_kernel,
+        out_shape=(
+            jax.ShapeDtypeStruct(sky, jnp.bfloat16),
+            jax.ShapeDtypeStruct(index, jnp.float32),
+            jax.ShapeDtypeStruct(blocks, jnp.bfloat16),
+        ),
+        in_specs=[pl.BlockSpec(memory_space=vmem)] * 3,
+        out_specs=(pl.BlockSpec(memory_space=vmem),) * 3,
+        scratch_shapes=[
+            vmem(sky, jnp.bfloat16),
+            vmem((NEAR, 2, STRIP), jnp.float32),
+            vmem(index, jnp.float32),
+            vmem(index, jnp.float32),
+            vmem((NEAR * PLANE, 4, STRIP), jnp.bfloat16),
+            vmem(blocks, jnp.bfloat16),
+            dma((2, PLANE)),
+            dma((2, NX)),
+            dma((2, NX)),
+            dma((2, NEAR)),
+            dma((2, PLANE)),
+            dma((2, NEAR)),
+            dma((2, 1)),
+        ],
+        compiler_params=pltpu.CompilerParams(collective_id=2, has_side_effects=True),
+        name="exchange",
+    )(start_piece, strips, visibilities)
 
 
 def reduce_kernel(
@@ -241,41 +453,36 @@
 
 
 def on_device(start_image, visibilities, strip_index, live_counts, uv_kernels):
-    observed, picked_ids, live_now = (
-        lax.all_to_all(
-            lax.all_to_all(array, "chan", split_axis=1, concat_axis=0, tiled=True),
-            "facet",
-            split_axis=2,
-            concat_axis=0,
-            tiled=True,
-        )
-        for array in (visibilities, owner_order(strip_index), live_counts)
-    )
-    chan_count = lax.axis_size("chan")
-    facet_count = lax.axis_size("facet")
-    slot_count = observed.shape[0]
-    chan_local = uv_kernels.shape[0]
-    uv_local = uv_kernels.shape[1]
-    all_channels = chan_local * chan_count
-    all_uvtiles = uv_local * facet_count
-    slab_rows = start_image.shape[0]
-    facet_width = start_image.shape[1]
-    strip_count = slab_rows * facet_width * facet_count // STRIP
-    step_size = strip_count / (2.5 * slot_count * all_channels * all_uvtiles)
+    slot_count = lax.axis_size("chan") * lax.axis_size("facet")
+    channels, uvtiles = visibilities.shape[1:3]
+    slab_rows, facet_width = start_image.shape
+    strip_count = OWNERS * PIECE
+    chan_local, uv_local = uv_kernels.shape[:2]
+    step_size = strip_count / (2.5 * slot_count * channels * uvtiles)
+
     lane_ids = jnp.arange(2 * VISB, dtype=jnp.int32) % VISB
-    live_mask = lane_ids < live_now[..., None]
-    flat_ids = picked_ids.reshape(-1)
+    live_mask = lane_ids < live_counts[..., None]
+    marked = jnp.where(live_mask, visibilities, jnp.bfloat16(FLAGGED))
+    marked = marked.reshape(NY, NX, 2, NZ, 2, 2, STRIP).transpose(4, 1, 0, 3, 2, 5, 6)
+    strips = owner_order(strip_index).astype(jnp.float32)
+    strips = strips.reshape(NY, NX, 2, NZ, 2, 2).transpose(4, 1, 0, 3, 2, 5)
     pieces = start_image.reshape(NY * NX, PIECE, STRIP)
     estimate = lax.dynamic_index_in_dim(pieces, lax.axis_index("chan"), 0, keepdims=False)
-    sky = lax.all_gather(start_image.astype(jnp.bfloat16), "facet", axis=0, tiled=False)
-    sky = sky.reshape(NZ, 2, NY, NX, 2, 4, STRIP).transpose(1, 3, 2, 0, 4, 5, 6)
+    sky, picked, observed = exchange(
+        estimate.astype(jnp.bfloat16),
+        strips.reshape(NEAR, 2, STRIP),
+        marked.reshape(OWNERS, 4, STRIP),
+    )
+    picked_ids = picked[:, 0, : 4 * NEAR].astype(jnp.int32).reshape(slot_count, chan_local, uv_local, TERMS)
+    flat_ids = picked_ids.reshape(-1)
+    observed = observed.reshape(slot_count, chan_local, uv_local, 2 * VISB)
     for iteration in range(ITERS):
         sky_strips = sky.reshape(strip_count, STRIP)
         gathered = sky_strips[picked_ids].reshape(slot_count, chan_local, uv_local, TERMS * STRIP)
         predicted = jnp.einsum(
             "scup,cupq->scuq", gathered, uv_kernels, preferred_element_type=jnp.float32
         )
-        residual = jnp.where(live_mask, predicted - observed.astype(jnp.float32), 0.0).astype(
+        residual = jnp.where(observed < FLAGGED, predicted - observed.astype(jnp.float32), 0.0).astype(
             jnp.bfloat16
         )
         adjoint = jnp.einsum(

time: 262 us -> 204 us (0.78)
  waiting for transfers between devices: 53.6 us -> 0 us
  Pallas kernels: 86.2 us -> 138 us
  starting transfers between devices: 37.3 us -> 0 us
  between operations: 13.7 us -> 0.22 us
  blocking collectives: 9.83 us -> 0 us
    pallas_call x0 -> x1, Pallas kernels: none -> 51.4 us  [exchange(): pl.pallas_call(exchange_kernel, out_shape=(jax.ShapeDtypeStruct(sky, jnp....]
    all_to_all x5 -> x0, starting transfers between devices: 37.3 us -> none  [the longest x2 19.1 us: on_device(): lax.all_to_all(lax.all_to_all(array, 'chan', split_axis=1, concat_axis=0,...]
    all_to_all x5 -> x0, waiting for transfers between devices: 34.5 us -> none  [the longest x3 27.3 us: on_device(): lax.all_to_all(array, 'chan', split_axis=1, concat_axis=0, tiled=True)]
    all_gather x1 -> x0, waiting for transfers between devices: 19.1 us -> none  [on_device(): lax.all_gather(start_image.astype(jnp.bfloat16), 'facet', axis=0, tiled=F...]
    all_to_all x1 -> x0, blocking collectives: 9.83 us -> none  [on_device(): lax.all_to_all(lax.all_to_all(array, 'chan', split_axis=1, concat_axis=0,...]
    all_to_all x9 -> x0, local copies, waits for them, and re-layouts: 2.79 us -> none  [the longest x3 1.86 us: on_device(): lax.all_to_all(array, 'chan', split_axis=1, concat_axis=0, tiled=True)]
  transfers between devices with their start and end apart: 6 -> 0, of which waited for: 5 -> 0; matrix products, arithmetic and copies ran while one was open for 7% -> 0% of each run, Pallas kernels for 0% -> 0%
where the time goes in v2:
time: 204 us; the launch traced here: 203 us
  Pallas kernels  138 us (68%)
  other arithmetic  32.9 us (16%)
  local copies, waits for them, and re-layouts  30.2 us (15%)
  matrix products  2.11 us (1%)
    pallas_call x2, Pallas kernels, reduce_step(): pl.pallas_call(body, out_shape=(out, jax.ShapeDtypeStruct((PIECE, STRIP),...  86.4 us
    pallas_call x1, Pallas kernels, exchange(): pl.pallas_call(exchange_kernel, out_shape=(jax.ShapeDtypeStruct(sky, jnp....  51.4 us
    scatter-add x2, other arithmetic, on_device(): gradient = jnp.zeros((strip_count, STRIP), jnp.float32).at[flat_ids].add(...  24.5 us
    gather x2, local copies, waits for them, and re-layouts, on_device(): sky_strips[picked_ids]  13.2 us

profile of v2, /device:TPU:1, one launch (start us, length us, event | category | flops | bytes accessed | tf_op | source)
XLA Modules:
  0.0 203.2 jit_solution(14916931653506899981)
XLA Ops:
  0.0 0.0 copy-start
  0.0 1.0 fusion.34
  1.1 0.8 copy.17
  1.8 0.9 reshape.165
  2.8 0.6 fusion.38
  3.4 1.2 compare_select_fusion.1
  4.6 0.1 reshape.168
  4.7 1.2 copy.18
  6.0 0.7 reshape.166
  6.7 1.7 copy.16
  8.3 0.2 reshape.167
  8.6 0.7 copy.19.meta_ref
  9.2 51.4 %exchange.1 = (bf16[512,8,128]{2,1,0:T(8,128)(2,1)}, f32[64,1,128]{2,1,0:T(1,128)}, bf16[64,8,4,128]{3,2,1,0:T(4,128)(2,1)}) custom-call(bf16[8,128]{1,0:T(8,128)(2,1)} %get-tuple-element.17.start_ref, f32[8,2,128]{2,1,0:T(2,128)} %copy.19.meta_ref, bf16[512,4,128]{2,1,0:T(4,128)(2,1)} %bitcast.91), custom_call_target="tpu_custom_call" | custom-call | tf_op jit(solution)/shard_map/exchange/pallas_call | solution.py:206
  60.6 0.0 copy-start.1
  60.6 0.9 fusion.37
  61.6 0.1 convert_element_type.68
  61.7 0.8 slice_convert_fusion
  62.5 1.4 broadcast_compare_fusion
  63.8 1.2 lt.107
  65.0 0.8 convert_element_type.69
  65.8 0.3 compare_select_fusion
  66.1 0.6 reshape.185
  66.7 0.0 copy-done.1
  66.7 0.0 copy-start.2
  66.7 6.2 %gather_fusion = bf16[2048,128]{1,0:T(8,128)(2,1)S(1)} fusion(bf16[4096,128]{1,0:T(8,128)(2,1)S(1)} %bitcast.89, s32[2048]{0:T(1024)S(1)} %broadcast_clamp_fusion), kind=kCustom, calls=%fused_computation | custom fusion | bytes 1056768 | tf_op jit(solution)/shard_map/gather | solution.py:481
  72.9 1.1 reshape.171
  74.1 0.0 copy-done.2
  74.1 0.6 reshape.182
  74.7 0.0 copy-done
  74.7 1.6 convolution_bitcast_fusion.2
  76.4 0.8 copy.23
  77.2 1.8 reshape.203
  79.0 12.5 %scatter_custom_fusion = f32[4096,128]{1,0:T(8,128)S(1)} fusion(s32[2048]{0:T(1024)S(1)} %bitcast.95, f32[2048,128]{1,0:T(8,128)} %reshape.203, f32[]{:T(128)} %constant.115.clone.1), kind=kCustom, calls=%fused_computation.21 | custom fusion | flops 262144 | bytes 2097664 | tf_op jit(solution)/shard_map/scatter-add | solution.py:494
  91.6 1.1 convert_bitcast_fusion.1.refs_0_
  92.7 49.4 %reduce_sky.1 = (bf16[512,8,128]{2,1,0:T(8,128)(2,1)}, f32[8,128]{1,0:T(8,128)}) custom-call(bf16[512,8,128]{2,1,0:T(8,128)(2,1)} %convert_bitcast_fusion.1.refs_0_, f32[8,128]{1,0:T(8,128)} %get-tuple-element.18.refs_1_), custom_call_target="tpu_custom_call" | custom-call | tf_op jit(solution)/shard_map/reduce_sky/pallas_call | solution.py:421
  142.0 0.0 copy-start.3
  142.1 7.0 %gather_fusion.1 = bf16[2048,128]{1,0:T(8,128)(2,1)S(1)} fusion(bf16[4096,128]{1,0:T(8,128)(2,1)} %bitcast.90, s32[2048]{0:T(1024)S(1)} %broadcast_clamp_fusion), kind=kCustom, calls=%fused_computation.1 | custom fusion | bytes 1056768 | tf_op jit(solution)/shard_map/gather | solution.py:481
  149.1 0.3 reshape.177
  149.4 0.0 copy-done.3
  149.4 0.5 convolution_bitcast_fusion
  149.9 0.8 copy.27
  150.7 0.8 reshape.211
  151.6 12.0 %scatter_custom_fusion.1 = f32[4096,128]{1,0:T(8,128)S(1)} fusion(s32[2048]{0:T(1024)S(1)} %bitcast.96, f32[2048,128]{1,0:T(8,128)S(1)} %reshape.211, f32[]{:T(128)} %constant.115.clone.1), kind=kCustom, calls=%fused_computation.19 | custom fusion | flops 262144 | bytes 2097156 | tf_op jit(solution)/shard_map/scatter-add | solution.py:494
  163.5 1.1 convert_bitcast_fusion.refs_0_
  164.6 37.0 %reduce_final.1 = (f32[32,8,128]{2,1,0:T(8,128)}, f32[8,128]{1,0:T(8,128)}) custom-call(bf16[512,8,128]{2,1,0:T(8,128)(2,1)} %convert_bitcast_fusion.refs_0_, f32[8,128]{1,0:T(8,128)} %get-tuple-element.15.refs_1_), custom_call_target="tpu_custom_call" | custom-call | tf_op jit(solution)/shard_map/reduce_final/pallas_call | solution.py:421
  201.6 1.6 reshape.181
  (4 shorter events, 0.0 us)
Async XLA Ops:
  0.0 74.7 %copy-start = (bf16[2,1,256,256]{3,2,1,0:T(8,128)(2,1)S(1)}, bf16[2,1,256,256]{3,2,1,0:T(8,128)(2,1)}, u32[]{:S(2)}) copy-start(bf16[2,1,256,256]{3,2,1,0:T(8,128)(2,1)} %param.9) | copy-start | bytes 786436
  60.6 6.1 %copy-start.1 = (bf16[512,8,128]{2,1,0:T(8,128)(2,1)S(1)}, bf16[512,8,128]{2,1,0:T(8,128)(2,1)}, u32[]{:S(2)}) copy-start(bf16[512,8,128]{2,1,0:T(8,128)(2,1)} %get-tuple-element.13) | copy-start | bytes 3145732
  66.7 7.3 %copy-start.2 = (bf16[64,8,4,128]{3,2,1,0:T(4,128)(2,1)S(1)}, bf16[64,8,4,128]{3,2,1,0:T(4,128)(2,1)}, u32[]{:S(2)}) copy-start(bf16[64,8,4,128]{3,2,1,0:T(4,128)(2,1)} %get-tuple-element.12) | copy-start | bytes 1572868
  142.0 7.4 %copy-start.3 = (pred[512,2,1,256]{3,1,0,2:T(4,128)(4,1)S(1)}, pred[512,2,1,256]{3,1,0,2:T(4,128)(4,1)}, u32[]{:S(2)}) copy-start(pred[512,2,1,256]{3,1,0,2:T(4,128)(4,1)} %lt.107) | copy-start | bytes 786436

commit v3 on v2

--- a/solution.py
+++ b/solution.py
@@ -182,7 +182,7 @@
     for dx in range(NX):
         spread_pair(dx).wait()
     sky_out[...] = sky[...]
-    index_out[...] = index_in[...]
+    index_out[...] = index_in[...].astype(jnp.int32)
     arrived = vis_in.at[pl.ds(1, PLANE - 1)]
     copy(arrived, arrived, vis_plane, 0, near(NX)[1]).wait()
     vis_out[...] = vis_in[...]
@@ -207,7 +207,7 @@
         exchange_kernel,
         out_shape=(
             jax.ShapeDtypeStruct(sky, jnp.bfloat16),
-            jax.ShapeDtypeStruct(index, jnp.float32),
+            jax.ShapeDtypeStruct(index, jnp.int32),
             jax.ShapeDtypeStruct(blocks, jnp.bfloat16),
         ),
         in_specs=[pl.BlockSpec(memory_space=vmem)] * 3,
@@ -442,6 +442,68 @@
     )(gradient, estimate)
 
 
+def gradient_kernel(index_ref, sky_ref, vis_ref, kernel_ref, out_ref, strips, picked, adjoint, *sums):
+    @pl.loop(0, OWNERS // 8)
+    def _(i):
+        block = sky_ref[pl.ds(i * 8, 8)].astype(jnp.float32)
+        strips[pl.ds(pl.multiple_of(i * 64, 64), 64)] = block.reshape(64, STRIP)
+        for total in sums:
+            total[pl.ds(pl.multiple_of(i * 64, 64), 64)] = jnp.zeros((64, STRIP), jnp.float32)
+
+    @pl.loop(0, PLANE)
+    def _(k):
+        for i in range(NEAR):
+            for q in range(4):
+                strip = index_ref[k, 0, 4 * i + q]
+                picked[q, k, pl.ds(i, 1)] = strips[pl.ds(strip, 1)]
+
+    for ch in range(2):
+        weights = kernel_ref[ch, 0]
+        gathered = jnp.concatenate(
+            [picked[2 * ch + j].reshape(PLANE * NEAR, STRIP).astype(jnp.bfloat16) for j in range(TERMS)], axis=1
+        )
+        predicted = jnp.dot(gathered, weights, preferred_element_type=jnp.float32)
+        observed = vis_ref[ch].astype(jnp.float32)
+        residual = jnp.where(observed < FLAGGED, predicted - observed, 0.0).astype(jnp.bfloat16)
+        back = lax.dot_general(residual, weights, (((1,), (1,)), ((), ())), preferred_element_type=jnp.float32)
+        for j in range(TERMS):
+            adjoint[2 * ch + j] = back[:, j * STRIP : (j + 1) * STRIP].reshape(PLANE, NEAR, STRIP)
+
+    @pl.loop(0, PLANE)
+    def _(k):
+        for i in range(NEAR):
+            for q in range(4):
+                total = sums[(4 * i + q) % len(sums)]
+                strip = index_ref[k, 0, 4 * i + q]
+                total[pl.ds(strip, 1)] += adjoint[q, k, pl.ds(i, 1)]
+
+    @pl.loop(0, OWNERS // 8)
+    def _(i):
+        rows = pl.ds(pl.multiple_of(i * 64, 64), 64)
+        block = sums[0][rows]
+        for total in sums[1:]:
+            block += total[rows]
+        out_ref[pl.ds(i * 8, 8)] = block.reshape(8, 8, STRIP).astype(jnp.bfloat16)
+
+
+SUMS = 8
+
+
+def gradient_step(index, sky, visibilities, kernels):
+    vmem = pltpu.VMEM
+    image = (OWNERS * PIECE, STRIP)
+    rows = (4, PLANE, NEAR, STRIP)
+    return pl.pallas_call(
+        gradient_kernel,
+        out_shape=jax.ShapeDtypeStruct((OWNERS, PIECE, STRIP), jnp.bfloat16),
+        in_specs=[pl.BlockSpec(memory_space=pltpu.SMEM)] + [pl.BlockSpec(memory_space=vmem)] * 3,
+        out_specs=pl.BlockSpec(memory_space=vmem),
+        scratch_shapes=[vmem(image, jnp.float32), vmem(rows, jnp.float32), vmem(rows, jnp.float32)]
+        + [vmem(image, jnp.float32)] * SUMS,
+        name="gradient",
+    )(index, sky, visibilities, kernels)
+
+
 def owner_order(strip):
     quarter = strip % 4
     core = strip // 4 % 2
@@ -457,7 +519,6 @@
     channels, uvtiles = visibilities.shape[1:3]
     slab_rows, facet_width = start_image.shape
     strip_count = OWNERS * PIECE
-    chan_local, uv_local = uv_kernels.shape[:2]
     step_size = strip_count / (2.5 * slot_count * channels * uvtiles)
 
     lane_ids = jnp.arange(2 * VISB, dtype=jnp.int32) % VISB
@@ -473,27 +534,9 @@
         strips.reshape(NEAR, 2, STRIP),
         marked.reshape(OWNERS, 4, STRIP),
     )
-    picked_ids = picked[:, 0, : 4 * NEAR].astype(jnp.int32).reshape(slot_count, chan_local, uv_local, TERMS)
-    flat_ids = picked_ids.reshape(-1)
-    observed = observed.reshape(slot_count, chan_local, uv_local, 2 * VISB)
+    observed = observed.reshape(slot_count, 2, 2 * VISB).swapaxes(0, 1)
     for iteration in range(ITERS):
-        sky_strips = sky.reshape(strip_count, STRIP)
-        gathered = sky_strips[picked_ids].reshape(slot_count, chan_local, uv_local, TERMS * STRIP)
-        predicted = jnp.einsum(
-            "scup,cupq->scuq", gathered, uv_kernels, preferred_element_type=jnp.float32
-        )
-        residual = jnp.where(observed < FLAGGED, predicted - observed.astype(jnp.float32), 0.0).astype(
-            jnp.bfloat16
-        )
-        adjoint = jnp.einsum(
-            "scuq,cupq->scup", residual, uv_kernels, preferred_element_type=jnp.float32
-        )
-        gradient = (
-            jnp.zeros((strip_count, STRIP), jnp.float32)
-            .at[flat_ids]
-            .add(adjoint.reshape(-1, STRIP))
-        )
-        gradient = gradient.astype(jnp.bfloat16).reshape(OWNERS, PIECE, STRIP)
+        gradient = gradient_step(picked, sky, observed, uv_kernels)
         sky, estimate = reduce_step(iteration == ITERS - 1, step_size, gradient, estimate)
     return sky.reshape(slab_rows, facet_width)
 

time: 204 us -> 171 us (0.84)
  other arithmetic: 32.9 us -> 2.14 us
  Pallas kernels: 138 us -> 157 us
  local copies, waits for them, and re-layouts: 30.2 us -> 11.3 us
  matrix products: 2.11 us -> 0 us
    scatter-add x2 -> x0, other arithmetic: 24.5 us -> none  [on_device(): gradient = jnp.zeros((strip_count, STRIP), jnp.float32).at[flat_ids].add(...]
    pallas_call x0 -> x2, Pallas kernels: none -> 19 us  [gradient_step(): pl.pallas_call(gradient_kernel, out_shape=jax.ShapeDtypeStruct((OWNERS, P...]
    gather x2 -> x0, local copies, waits for them, and re-layouts: 13.2 us -> none  [on_device(): sky_strips[picked_ids]]
    reshape x2 -> x0, other arithmetic: 2.19 us -> none  [on_device(): gradient = gradient.astype(jnp.bfloat16).reshape(OWNERS, PIECE, STRIP)]
    dot_general x2 -> x0, matrix products: 2.11 us -> none  [on_device(): jnp.einsum('scuq,cupq->scup', residual, uv_kernels, preferred_element_typ...]
where the time goes in v3:
time: 171 us; the launch traced here: 170 us
  Pallas kernels  157 us (92%)
  local copies, waits for them, and re-layouts  11.3 us (7%)
  other arithmetic  2.14 us (1%)
    pallas_call x2, Pallas kernels, reduce_step(): pl.pallas_call(body, out_shape=(out, jax.ShapeDtypeStruct((PIECE, STRIP),...  86.3 us
    pallas_call x1, Pallas kernels, exchange(): pl.pallas_call(exchange_kernel, out_shape=(jax.ShapeDtypeStruct(sky, jnp....  51.4 us
    pallas_call x2, Pallas kernels, gradient_step(): pl.pallas_call(gradient_kernel, out_shape=jax.ShapeDtypeStruct((OWNERS, P...  19 us

profile of v3, /device:TPU:1, one launch (start us, length us, event | category | flops | bytes accessed | tf_op | source)
XLA Modules:
  0.0 170.2 jit_solution(16442234696105526218)
XLA Ops:
  0.0 0.0 copy-start
  0.0 0.7 copy-done
  0.7 0.3 fusion.10
  1.0 0.0 copy-start.1
  1.0 0.7 copy-done.1
  1.7 0.1 copy.11
  1.8 0.9 reshape.39
  2.7 0.6 fusion.11
  3.3 1.2 compare_select_fusion
  4.6 0.1 reshape.42
  4.7 1.2 copy.12
  5.9 0.7 reshape.40
  6.6 1.7 copy.10
  8.3 0.2 reshape.41
  8.5 0.7 copy.13.meta_ref
  9.2 51.4 %exchange.1 = (bf16[512,8,128]{2,1,0:T(8,128)(2,1)}, s32[64,1,128]{2,1,0:T(1,128)}, bf16[64,8,4,128]{3,2,1,0:T(4,128)(2,1)}) custom-call(bf16[8,128]{1,0:T(8,128)(2,1)} %get-tuple-element.17.start_ref, f32[8,2,128]{2,1,0:T(2,128)} %copy.13.meta_ref, bf16[512,4,128]{2,1,0:T(4,128)(2,1)} %bitcast.21), custom_call_target="tpu_custom_call" | custom-call | tf_op jit(solution)/shard_map/exchange/pallas_call | solution.py:206
  60.5 1.9 %reshape.44 = bf16[512,2,256]{2,1,0:T(2,128)(2,1)S(1)} reshape(bf16[64,8,4,128]{3,2,1,0:T(4,128)(2,1)} %get-tuple-element.13) | data formatting | bytes 1048576 | tf_op jit(solution)/shard_map/reshape | solution.py:537
  62.5 0.9 copy.16
  63.3 9.5 %gradient.2.refs_0_ = bf16[512,8,128]{2,1,0:T(8,128)(2,1)} custom-call(s32[64,1,128]{2,1,0:T(1,128)} %get-tuple-element.11.index_ref, bf16[512,8,128]{2,1,0:T(8,128)(2,1)} %get-tuple-element.12.sky_ref, bf16[2,512,256]{2,1,0:T(8,128)(2,1)} %bitcast.19, bf16[2,1,256,256]{3,2,1,0:T(8,128)(2,1)} %kernel_ref.3), custom_call_target="tpu_custom_call" | custom-call | tf_op jit(solution)/shard_map/gradient/pallas_call | solution.py:496
  72.8 49.3 %reduce_sky.1 = (bf16[512,8,128]{2,1,0:T(8,128)(2,1)}, f32[8,128]{1,0:T(8,128)}) custom-call(bf16[512,8,128]{2,1,0:T(8,128)(2,1)} %gradient.2.refs_0_, f32[8,128]{1,0:T(8,128)} %get-tuple-element.18.refs_1_), custom_call_target="tpu_custom_call" | custom-call | tf_op jit(solution)/shard_map/reduce_sky/pallas_call | solution.py:421
  122.2 9.5 %gradient.3.refs_0_ = bf16[512,8,128]{2,1,0:T(8,128)(2,1)} custom-call(s32[64,1,128]{2,1,0:T(1,128)} %get-tuple-element.11.index_ref, bf16[512,8,128]{2,1,0:T(8,128)(2,1)} %get-tuple-element.14.sky_ref, bf16[2,512,256]{2,1,0:T(8,128)(2,1)} %bitcast.20, bf16[2,1,256,256]{3,2,1,0:T(8,128)(2,1)} %kernel_ref.3), custom_call_target="tpu_custom_call" | custom-call | tf_op jit(solution)/shard_map/gradient/pallas_call | solution.py:496
  131.6 37.0 %reduce_final.1 = (f32[32,8,128]{2,1,0:T(8,128)}, f32[8,128]{1,0:T(8,128)}) custom-call(bf16[512,8,128]{2,1,0:T(8,128)(2,1)} %gradient.3.refs_0_, f32[8,128]{1,0:T(8,128)} %get-tuple-element.15.refs_1_), custom_call_target="tpu_custom_call" | custom-call | tf_op jit(solution)/shard_map/reduce_final/pallas_call | solution.py:421
  168.6 1.6 reshape.45
  (2 shorter events, 0.0 us)
Async XLA Ops:
  0.0 0.7 copy-start
  1.0 0.7 copy-start.1

commit v4 on v3

v4 whole, which is shorter than its diff:
```python
import jax
import jax.numpy as jnp
from jax import lax
from jax.experimental import pallas as pl
from jax.experimental.pallas import tpu as pltpu
from jax.sharding import PartitionSpec as P

STRIP = 128
VISB = 128
TERMS = 2
ITERS = 2
NX = 4
NY = 8
NZ = 8
PLANE = NY * NZ
OWNERS = 2 * NX * PLANE
PIECE = 8
NEAR = 2 * NX

FLAGGED = 1024.0

shrinkage = 0.05
MESH = pl.DeviceIdType.MESH


class Place:
    def __init__(self):
        chan = lax.axis_index("chan")
        facet = lax.axis_index("facet")
        self.chan, self.facet = chan, facet
        self.y, self.x = chan // NX, chan % NX
        self.z, self.core = facet // 2, facet % 2
        self.spot = self.y * NZ + self.z
        self.owner = self.core * NX + self.x
        self.ys = [lax.rem(self.y + d, NY) for d in range(NY)]
        self.zs = [lax.rem(self.z + d, NZ) for d in range(NZ)]
        self.xs = [lax.rem(self.x + d, NX) for d in range(NX)]
        self.chan_y = [yy * NX + self.x for yy in self.ys]
        self.facet_z = [zz * 2 + self.core for zz in self.zs]
        self.partner = (chan, self.z * 2 + (1 - self.core))

    def on_x(self, dx):
        return (self.y * NX + self.xs[dx], self.facet)

    def on_plane(self, dy, dz):
        return self.ys[dy] * NZ + self.zs[dz], (self.chan_y[dy], self.facet_z[dz])

    def on_chan(self, dy, dx):
        return (self.ys[dy] * NX + self.xs[dx], self.facet)

    def near(self, i):
        core = lax.rem(self.core + lax.rem(i, 2), 2)
        step = i // 2
        xx = lax.rem(self.x + step * (step + 1) // 2, NX)
        return core * NX + xx, (self.y * NX + xx, self.z * 2 + core)


def reach(d, length):
    return min(d, length - d)


FAR_FIRST = sorted(
    ((dy, dz) for dy in range(NY) for dz in range(NZ) if dy or dz),
    key=lambda step: -reach(step[0], NY) - reach(step[1], NZ),
)
CHAN_FAR_FIRST = sorted(
    ((dy, dx) for dy in range(NY) for dx in range(NX) if dy or dx),
    key=lambda step: -reach(step[0], NY) - reach(step[1], NX),
)


def remote(src, dst, sems, at, target):
    return pltpu.make_async_remote_copy(
        src_ref=src,
        dst_ref=dst,
        send_sem=sems.at[0, at],
        recv_sem=sems.at[1, at],
        device_id=target,
        device_id_type=MESH,
    )


def greet(targets):
    barrier = pltpu.get_barrier_semaphore()
    for target in targets:
        pl.semaphore_signal(barrier, inc=1, device_id=target, device_id_type=MESH)
    pl.semaphore_wait(barrier, len(targets))


def exchange_kernel(
    start_ref,
    meta_ref,
    vis_ref,
    sky_out,
    index_out,
    vis_out,
    sky,
    meta1,
    packed,
    index_in,
    vis1,
    vis_in,
    sky_plane,
    sky_x,
    sky_pair,
    meta_near,
    meta_plane,
    vis_near,
    vis_plane,
    own_sem,
):
    me = Place()
    own_sky = sky.at[me.owner * PLANE + me.spot]
    sky_copy = pltpu.make_async_copy(start_ref, own_sky, own_sem.at[0])
    sky_copy.start()
    vis_copy = pltpu.make_async_copy(
        vis_ref.at[pl.ds(me.owner * PLANE, PLANE)], vis1.at[pl.ds(0, PLANE)], own_sem.at[1]
    )
    vis_copy.start()
    greet([me.on_plane(dy, dz)[1] for dy, dz in FAR_FIRST] + [me.near(i)[1] for i in range(1, NEAR)])

    for dy, dz in FAR_FIRST:
        remote(start_ref, own_sky, sky_plane, 0, me.on_plane(dy, dz)[1]).start()

    def near_meta(i):
        return remote(meta_ref, meta1.at[i], meta_near, i, me.near(i)[1])

    def near_vis(i):
        owner, target = me.near(i)
        block = vis_ref.at[pl.ds(owner * PLANE, PLANE)]
        return remote(block, vis1.at[pl.ds(i * PLANE, PLANE)], vis_near, i, target)

    def own_block(xx):
        return sky.at[pl.ds((me.core * NX + xx) * PLANE, PLANE)]

    def spread_x(dx):
        return remote(own_block(me.x), own_block(me.x), sky_x, dx, me.on_x(dx))

    def spread_pair(dx):
        block = own_block(me.xs[dx])
        return remote(block, block, sky_pair, dx, me.partner)

    for i in range(1, NEAR):
        near_meta(i).start()
    for i in range(1, NEAR):
        near_vis(i).start()

    sky_copy.wait()
    vis_copy.wait()

    def forward(i):
        base = i * PLANE
        vis_in[0, i] = vis1[base + me.spot]
        for dy, dz in FAR_FIRST:
            place, target = me.on_plane(dy, dz)
            remote(vis1.at[base + place], vis_in.at[dy * NZ + dz, i], vis_plane, 0, target).start()

    forward(0)

    for i in range(1, NEAR):
        near_meta(i).wait_recv()
    lane = lax.broadcasted_iota(jnp.int32, (PLANE, STRIP), 1)
    place = lax.broadcasted_iota(jnp.int32, (PLANE, STRIP), 0)
    belongs = (lane // 2) == (place // NZ) * NX + me.x
    column = lax.broadcasted_iota(jnp.int32, (STRIP, STRIP), 1)
    source = lax.broadcasted_iota(jnp.int32, (STRIP, STRIP), 0)
    total = jnp.zeros((2 * PLANE, STRIP), jnp.float32)
    for i in range(NEAR):
        held = meta_ref if i == 0 else meta1.at[i]
        for j in range(TERMS):
            strips = held[pl.ds(me.core * 2 + j, NZ, stride=4)]
            high = strips // 64
            low = strips - 64 * high
            spread = jnp.concatenate(
                [
                    jnp.where(belongs, jnp.concatenate([part.astype(jnp.float32)] * NY, axis=0), 0.0)
                    for part in (high, low)
                ],
                axis=0,
            )
            move = jnp.where(column == 4 * i + 2 * (source % 2) + j, 1.0, 0.0).astype(jnp.bfloat16)
            total += jnp.dot(spread.astype(jnp.bfloat16), move, preferred_element_type=jnp.float32)
    rows = 64.0 * total[:PLANE] + total[PLANE:]
    for d in range(PLANE):
        packed[d] = rows[d : d + 1]
    index_in[0] = packed[me.spot]
    for dy, dz in FAR_FIRST:
        spot, target = me.on_plane(dy, dz)
        remote(packed.at[spot], index_in.at[dy * NZ + dz], meta_plane, 0, target).start()

    near_vis(1).wait_recv()
    forward(1)

    others = sky.at[pl.ds(0, PLANE - 1)]
    remote(others, others, sky_plane, 0, me.partner).wait_recv()
    for dx in (2, 1, 3):
        spread_x(dx).start()
    spread_pair(0).start()

    @pl.loop(2, NEAR)
    def _(i):
        near_vis(i).wait_recv()
        forward(i)

    for dx in (1, 3, 2):
        spread_x(dx).wait_recv()
        spread_pair(NX - dx).start()
    far_index = index_in.at[pl.ds(1, PLANE - 1)]
    remote(far_index, far_index, meta_plane, 0, me.partner).wait()
    index_out[...] = index_in[...].astype(jnp.int32)
    for dx in range(NX):
        spread_pair(dx).wait()
    sky_out[...] = sky[...]
    for dx in (1, 3, 2):
        spread_x(dx).wait_send()
    for i in range(1, NEAR):
        near_meta(i).wait_send()
        near_vis(i).wait_send()
    remote(others, others, sky_plane, 0, me.partner).wait_send()
    arrived = vis_in.at[pl.ds(1, PLANE - 1)]
    remote(arrived, arrived, vis_plane, 0, me.partner).wait()
    vis_out[...] = vis_in[...]


def exchange(start_piece, strips, visibilities):
    dma = pltpu.SemaphoreType.DMA
    vmem = pltpu.VMEM
    sky = (OWNERS, PIECE, STRIP)
    index = (PLANE, 1, STRIP)
    blocks = (PLANE, NEAR, 4, STRIP)
    return pl.pallas_call(
        exchange_kernel,
        out_shape=(
            jax.ShapeDtypeStruct(sky, jnp.bfloat16),
            jax.ShapeDtypeStruct(index, jnp.int32),
            jax.ShapeDtypeStruct(blocks, jnp.bfloat16),
        ),
        in_specs=[pl.BlockSpec(memory_space=vmem)] * 3,
        out_specs=(pl.BlockSpec(memory_space=vmem),) * 3,
        scratch_shapes=[
            vmem(sky, jnp.bfloat16),
            vmem((NEAR, NZ * 4, STRIP), jnp.int32),
            vmem(index, jnp.float32),
            vmem(index, jnp.float32),
            vmem((NEAR * PLANE, 4, STRIP), jnp.bfloat16),
            vmem(blocks, jnp.bfloat16),
            dma((2, 1)),
            dma((2, NX)),
            dma((2, NX)),
            dma((2, NEAR)),
            dma((2, 1)),
            dma((2, NEAR)),
            dma((2, 1)),
            dma((2,)),
        ],
        compiler_params=pltpu.CompilerParams(collective_id=2, has_side_effects=True),
        name="exchange",
    )(start_piece, strips, visibilities)


def reduce_kernel(
    final, step_size, g_ref, est_ref, out_ref, est_out, got1, sum1, got2, sum2, got3, sky, sems1, sems2, sems3, sems4, sems5, sems6
):
    me = Place()
    targets = [me.on_plane(dy, dz)[1] for dy, dz in FAR_FIRST]
    if final:
        targets += [me.on_chan(dy, dx) for dy, dx in CHAN_FAR_FIRST if dy and dx]
    greet(targets + [me.on_x(dx) for dx in (2, 1, 3)] + [me.partner])

    order = [1, 3, 2, 0]

    def own_block(xx):
        return pl.ds((me.core * NX + xx) * PLANE, PLANE)

    def pair_copy(dx):
        block = g_ref.at[pl.ds(((1 - me.core) * NX + me.xs[dx]) * PLANE, PLANE)]
        return remote(block, got1.at[dx], sems1, dx, me.partner)

    for dx in order:
        pair_copy(dx).start()

    def x_copy(dx):
        return remote(sum1.at[dx], got2.at[dx], sems2, dx, me.on_x(dx))

    for dx in order[:-1]:
        pair_copy(dx).wait_recv()
        base = (me.core * NX + me.xs[dx]) * PLANE

        @pl.loop(0, PLANE // 8)
        def _(i):
            total = g_ref[pl.ds(base + i * 8, 8)].astype(jnp.float32) + got1[dx, pl.ds(i * 8, 8)].astype(jnp.float32)
            sum1[dx, pl.ds(i * 8, 8)] = total.astype(jnp.bfloat16)

        x_copy(dx).start()
    pair_copy(0).wait_recv()
    for dx in order[:-1]:
        x_copy(dx).wait_recv()
    base = me.owner * PLANE

    @pl.loop(0, PLANE // 8)
    def _(i):
        rows = pl.ds(i * 8, 8)
        total = g_ref[pl.ds(base + i * 8, 8)].astype(jnp.float32) + got1[0, rows].astype(jnp.float32)
        for dx in order[:-1]:
            total += got2[dx, rows].astype(jnp.float32)
        sum2[rows] = total.astype(jnp.bfloat16)

    for dy, dz in FAR_FIRST:
        place, target = me.on_plane(dy, dz)
        remote(sum2.at[place], got3.at[dy * NZ + dz], sems3, 0, target).start()
    others = got3.at[pl.ds(1, PLANE - 1)]
    all_plane = remote(others, others, sems3, 0, me.partner)
    all_plane.wait_recv()

    parts = [sum2[me.spot].astype(jnp.float32)] + [jnp.zeros((PIECE, STRIP), jnp.float32) for _ in range(3)]
    for k in range(1, PLANE):
        parts[k % 4] += got3[k].astype(jnp.float32)
    gradient = (parts[0] + parts[1]) + (parts[2] + parts[3])
    estimate = jnp.maximum(est_ref[...] - step_size * gradient - shrinkage, 0.0)

    if final:
        mine = sky.at[pl.ds(pl.multiple_of(me.chan * PIECE, PIECE), PIECE)]
        mine[...] = estimate
        for dy, dx in CHAN_FAR_FIRST:
            remote(mine, mine, sems4, 0, me.on_chan(dy, dx)).start()
        est_out[...] = estimate
        rest = sky.at[pl.ds(0, (NY * NX - 1) * PIECE)]
        remote(rest, rest, sems4, 0, me.partner).wait()
        for quarter in range(4):
            out_ref[:, quarter * STRIP : (quarter + 1) * STRIP] = sky[pl.ds(quarter, 2 * NY * NX, stride=4)]
    else:
        mine = sky.at[me.owner * PLANE + me.spot]
        mine[...] = estimate.astype(jnp.bfloat16)
        for dy, dz in FAR_FIRST:
            remote(mine, mine, sems4, 0, me.on_plane(dy, dz)[1]).start()
        est_out[...] = estimate
        rest = sky.at[pl.ds(0, PLANE - 1)]
        all_sky = remote(rest, rest, sems4, 0, me.partner)
        all_sky.wait_recv()

        def spread_x(dx):
            block = sky.at[own_block(me.x)]
            return remote(block, block, sems5, dx, me.on_x(dx))

        def spread_pair(dx):
            block = sky.at[own_block(me.xs[dx])]
            return remote(block, block, sems6, dx, me.partner)

        for dx in (2, 1, 3):
            spread_x(dx).start()
        spread_pair(0).start()
        for dx in order[:-1]:
            spread_x(dx).wait_recv()
            spread_pair(NX - dx).start()
        for dx in range(NX):
            spread_pair(dx).wait()
        out_ref[...] = sky[...]
        for dx in order[:-1]:
            spread_x(dx).wait_send()
        all_sky.wait_send()

    for dx in order:
        pair_copy(dx).wait_send()
    for dx in order[:-1]:
        x_copy(dx).wait_send()
    all_plane.wait_send()


def reduce_step(final, step_size, gradient, estimate):
    def body(*refs):
        reduce_kernel(final, step_size, *refs)

    dma = pltpu.SemaphoreType.DMA
    if final:
        out = jax.ShapeDtypeStruct((2 * NY * NX, 4 * STRIP), jnp.float32)
        sky = pltpu.VMEM((NY * NX * PIECE, STRIP), jnp.float32)
    else:
        sky = pltpu.VMEM((OWNERS, PIECE, STRIP), jnp.bfloat16)
        out = jax.ShapeDtypeStruct((OWNERS, PIECE, STRIP), jnp.bfloat16)
    return pl.pallas_call(
        body,
        out_shape=(out, jax.ShapeDtypeStruct((PIECE, STRIP), jnp.float32)),
        in_specs=[pl.BlockSpec(memory_space=pltpu.VMEM)] * 2,
        out_specs=(pl.BlockSpec(memory_space=pltpu.VMEM),) * 2,
        scratch_shapes=[
            pltpu.VMEM((NX, PLANE, PIECE, STRIP), jnp.bfloat16),
            pltpu.VMEM((NX, PLANE, PIECE, STRIP), jnp.bfloat16),
            pltpu.VMEM((NX, PLANE, PIECE, STRIP), jnp.bfloat16),
            pltpu.VMEM((PLANE, PIECE, STRIP), jnp.bfloat16),
            pltpu.VMEM((PLANE, PIECE, STRIP), jnp.bfloat16),
            sky,
            dma((2, NX)),
            dma((2, NX)),
            dma((2, 1)),
            dma((2, 1)),
            dma((2, NX)),
            dma((2, NX)),
        ],
        compiler_params=pltpu.CompilerParams(collective_id=1 if final else 0, has_side_effects=True),
        name="reduce_final" if final else "reduce_sky",
    )(gradient, estimate)


def gradient_kernel(index_ref, sky_ref, vis_ref, kernel_ref, out_ref, strips, picked, adjoint, *sums):
    @pl.loop(0, OWNERS // 8)
    def _(i):
        block = sky_ref[pl.ds(i * 8, 8)].astype(jnp.float32)
        strips[pl.ds(pl.multiple_of(i * 64, 64), 64)] = block.reshape(64, STRIP)
        for total in sums:
            total[pl.ds(pl.multiple_of(i * 64, 64), 64)] = jnp.zeros((64, STRIP), jnp.float32)

    @pl.loop(0, PLANE)
    def _(k):
        for i in range(NEAR):
            for q in range(4):
                strip = index_ref[k, 0, 4 * i + q]
                picked[q, k, pl.ds(i, 1)] = strips[pl.ds(strip, 1)]

    for ch in range(2):
        weights = kernel_ref[ch, 0]
        gathered = jnp.concatenate(
            [picked[2 * ch + j].reshape(PLANE * NEAR, STRIP).astype(jnp.bfloat16) for j in range(TERMS)], axis=1
        )
        predicted = jnp.dot(gathered, weights, preferred_element_type=jnp.float32)
        observed = vis_ref[ch].astype(jnp.float32)
        residual = jnp.where(observed < FLAGGED, predicted - observed, 0.0).astype(jnp.bfloat16)
        back = lax.dot_general(residual, weights, (((1,), (1,)), ((), ())), preferred_element_type=jnp.float32)
        for j in range(TERMS):
            adjoint[2 * ch + j] = back[:, j * STRIP : (j + 1) * STRIP].reshape(PLANE, NEAR, STRIP)

    @pl.loop(0, PLANE)
    def _(k):
        for i in range(NEAR):
            for q in range(4):
                total = sums[(4 * i + q) % len(sums)]
                strip = index_ref[k, 0, 4 * i + q]
                total[pl.ds(strip, 1)] += adjoint[q, k, pl.ds(i, 1)]

    @pl.loop(0, OWNERS // 8)
    def _(i):
        rows = pl.ds(pl.multiple_of(i * 64, 64), 64)
        block = sums[0][rows]
        for total in sums[1:]:
            block += total[rows]
        out_ref[pl.ds(i * 8, 8)] = block.reshape(8, 8, STRIP).astype(jnp.bfloat16)


SUMS = 8


def gradient_step(index, sky, visibilities, kernels):
    vmem = pltpu.VMEM
    image = (OWNERS * PIECE, STRIP)
    rows = (4, PLANE, NEAR, STRIP)
    return pl.pallas_call(
        gradient_kernel,
        out_shape=jax.ShapeDtypeStruct((OWNERS, PIECE, STRIP), jnp.bfloat16),
        in_specs=[pl.BlockSpec(memory_space=pltpu.SMEM)] + [pl.BlockSpec(memory_space=vmem)] * 3,
        out_specs=pl.BlockSpec(memory_space=vmem),
        scratch_shapes=[vmem(image, jnp.float32), vmem(rows, jnp.float32), vmem(rows, jnp.float32)]
        + [vmem(image, jnp.float32)] * SUMS,
        name="gradient",
    )(index, sky, visibilities, kernels)


def owner_order(strip):
    quarter = strip % 4
    core = strip // 4 % 2
    z = strip // 8 % 8
    low_row = strip // 64 % 2
    x = strip // 128 % 4
    y = strip // 512
    return (((core * NX + x) * NY + y) * NZ + z) * PIECE + low_row * 4 + quarter


def on_device(start_image, visibilities, strip_index, live_counts, uv_kernels):
    slot_count = lax.axis_size("chan") * lax.axis_size("facet")
    channels, uvtiles = visibilities.shape[1:3]
    slab_rows, facet_width = start_image.shape
    strip_count = OWNERS * PIECE
    step_size = strip_count / (2.5 * slot_count * channels * uvtiles)

    lane_ids = jnp.arange(2 * VISB, dtype=jnp.int32) % VISB
    live_mask = lane_ids < live_counts[..., None]
    marked = jnp.where(live_mask, visibilities, jnp.bfloat16(FLAGGED))
    marked = marked.reshape(NY, NX, 2, NZ, 2, 2, STRIP).transpose(4, 1, 0, 3, 2, 5, 6)
    strips = owner_order(strip_index).transpose(0, 2, 3, 1).reshape(NZ * 4, channels)
    strips = jnp.pad(strips, ((0, 0), (0, STRIP - channels)))
    rows = lax.dynamic_slice_in_dim(start_image, lax.axis_index("chan") * 2, 2, 0)
    estimate = rows.reshape(PIECE, STRIP)
    sky, picked, observed = exchange(
        estimate.astype(jnp.bfloat16),
        strips,
        marked.reshape(OWNERS, 4, STRIP),
    )
    observed = observed.reshape(slot_count, 2, 2 * VISB).swapaxes(0, 1)
    for iteration in range(ITERS):
        gradient = gradient_step(picked, sky, observed, uv_kernels)
        sky, estimate = reduce_step(iteration == ITERS - 1, step_size, gradient, estimate)
    return sky


def solution(mesh):
    placed = (
        P(None, "facet"),
        P(("chan", "facet"), None, None, None),
        P(("chan", "facet"), None, None, None),
        P(("chan", "facet"), None, None),
        P("chan", "facet", None, None),
    )
    return jax.shard_map(
        on_device, mesh=mesh, in_specs=placed, out_specs=P(None, "facet"), check_vma=False
    )
```

time: 171 us -> 140 us (0.82)
  Pallas kernels: 157 us -> 129 us
  local copies, waits for them, and re-layouts: 11.3 us -> 7.41 us
    pallas_call x2, Pallas kernels: 86.3 us -> 70.2 us  [reduce_step(): pl.pallas_call(body, out_shape=(out, jax.ShapeDtypeStruct((PIECE, STRIP),...]
    pallas_call x1, Pallas kernels: 51.4 us -> 40 us  [exchange(): pl.pallas_call(exchange_kernel, out_shape=(jax.ShapeDtypeStruct(sky, jnp....]
    reshape x5 -> x1, local copies, waits for them, and re-layouts: 4.05 us -> 0.01 us  [on_device(): estimate = rows.reshape(PIECE, STRIP)]
where the time goes in v4:
time: 140 us; the launch traced here: 139 us
  Pallas kernels  129 us (92%)
  local copies, waits for them, and re-layouts  7.41 us (5%)
  other arithmetic  2.11 us (2%)
    pallas_call x2, Pallas kernels, reduce_step(): pl.pallas_call(body, out_shape=(out, jax.ShapeDtypeStruct((PIECE, STRIP),...  70.2 us
    pallas_call x1, Pallas kernels, exchange(): pl.pallas_call(exchange_kernel, out_shape=(jax.ShapeDtypeStruct(sky, jnp....  40 us
    pallas_call x2, Pallas kernels, gradient_step(): pl.pallas_call(gradient_kernel, out_shape=jax.ShapeDtypeStruct((OWNERS, P...  19 us

profile of v4, /device:TPU:1, one launch (start us, length us, event | category | flops | bytes accessed | tf_op | source)
XLA Modules:
  0.0 138.8 jit_solution(13779986395354553287)
XLA Ops:
  0.0 0.0 copy-start
  0.0 0.0 copy-start.2
  0.0 0.9 copy-done
  0.9 0.0 copy-start.1
  0.9 0.6 convert_element_type.3.start_ref
  1.5 0.0 copy-done.2
  1.5 0.3 fusion.5
  1.8 0.0 copy-done.1
  1.8 0.0 copy-start.3
  1.8 0.6 pad.4.meta_ref
  2.4 0.1 copy-done.3
  2.5 0.1 copy.8
  2.6 1.2 compare_select_fusion
  3.8 0.1 reshape.35
  4.0 1.2 copy.9
  5.2 40.0 %exchange.1 = (bf16[512,8,128]{2,1,0:T(8,128)(2,1)}, s32[64,1,128]{2,1,0:T(1,128)}, bf16[64,8,4,128]{3,2,1,0:T(4,128)(2,1)}) custom-call(bf16[8,128]{1,0:T(8,128)(2,1)} %convert_element_type.3.start_ref, s32[32,128]{1,0:T(8,128)} %pad.4.meta_ref, bf16[512,4,128]{2,1,0:T(4,128)(2,1)} %bitcast.14), custom_call_target="tpu_custom_call" | custom-call | tf_op jit(solution)/shard_map/exchange/pallas_call | solution.py:231
  45.2 1.9 %reshape.37 = bf16[512,2,256]{2,1,0:T(2,128)(2,1)S(1)} reshape(bf16[64,8,4,128]{3,2,1,0:T(4,128)(2,1)} %get-tuple-element.13) | data formatting | bytes 1048576 | tf_op jit(solution)/shard_map/reshape | solution.py:496
  47.1 0.9 copy.12
  48.0 9.5 %gradient.2.refs_0_ = bf16[512,8,128]{2,1,0:T(8,128)(2,1)} custom-call(s32[64,1,128]{2,1,0:T(1,128)} %get-tuple-element.11.index_ref, bf16[512,8,128]{2,1,0:T(8,128)(2,1)} %get-tuple-element.12.sky_ref, bf16[2,512,256]{2,1,0:T(8,128)(2,1)} %bitcast.12, bf16[2,1,256,256]{3,2,1,0:T(8,128)(2,1)} %kernel_ref.3), custom_call_target="tpu_custom_call" | custom-call | tf_op jit(solution)/shard_map/gradient/pallas_call | solution.py:455
  57.5 42.1 %reduce_sky.1 = (bf16[512,8,128]{2,1,0:T(8,128)(2,1)}, f32[8,128]{1,0:T(8,128)}) custom-call(bf16[512,8,128]{2,1,0:T(8,128)(2,1)} %gradient.2.refs_0_, f32[8,128]{1,0:T(8,128)} %copy-done.1), custom_call_target="tpu_custom_call" | custom-call | tf_op jit(solution)/shard_map/reduce_sky/pallas_call | solution.py:380
  99.5 9.5 %gradient.3.refs_0_ = bf16[512,8,128]{2,1,0:T(8,128)(2,1)} custom-call(s32[64,1,128]{2,1,0:T(1,128)} %get-tuple-element.11.index_ref, bf16[512,8,128]{2,1,0:T(8,128)(2,1)} %get-tuple-element.14.sky_ref, bf16[2,512,256]{2,1,0:T(8,128)(2,1)} %bitcast.13, bf16[2,1,256,256]{3,2,1,0:T(8,128)(2,1)} %kernel_ref.3), custom_call_target="tpu_custom_call" | custom-call | tf_op jit(solution)/shard_map/gradient/pallas_call | solution.py:455
  109.1 28.1 %reduce_final.1 = (f32[64,512]{1,0:T(8,128)}, f32[8,128]{1,0:T(8,128)}) custom-call(bf16[512,8,128]{2,1,0:T(8,128)(2,1)} %gradient.3.refs_0_, f32[8,128]{1,0:T(8,128)} %get-tuple-element.15.refs_1_), custom_call_target="tpu_custom_call" | custom-call | tf_op jit(solution)/shard_map/reduce_final/pallas_call | solution.py:380
  137.2 1.6 %copy.14 = f32[64,512]{1,0:T(8,128)} copy(f32[64,512]{1,0:T(8,128)} %get-tuple-element.16) | data formatting | bytes 262144
  (3 shorter events, 0.0 us)
Async XLA Ops:
  0.0 0.9 copy-start
  0.0 1.5 %copy-start.2 = (s32[1,64,16,2]{1,3,2,0:T(2,128)S(1)}, s32[1,64,16,2]{1,3,2,0:T(2,128)}, u32[]{:S(2)}) copy-start(s32[1,64,16,2]{1,3,2,0:T(2,128)} %param.7) | copy-start | bytes 24580
  0.9 0.9 copy-start.1
  1.8 0.7 copy-start.3

commit v5 on v4

--- a/solution.py
+++ b/solution.py
@@ -16,6 +16,10 @@
 OWNERS = 2 * NX * PLANE
 PIECE = 8
 NEAR = 2 * NX
+GROUP = 4 * NEAR
+BLOCKS = PLANE * NEAR
+READS = 4 * BLOCKS
+HALF = 64
 
 FLAGGED = 1024.0
 
@@ -84,7 +88,7 @@
     barrier = pltpu.get_barrier_semaphore()
     for target in targets:
         pl.semaphore_signal(barrier, inc=1, device_id=target, device_id_type=MESH)
-    pl.semaphore_wait(barrier, len(targets))
+    return lambda: pl.semaphore_wait(barrier, len(targets))
 
 
 def exchange_kernel(
@@ -117,7 +121,7 @@
         vis_ref.at[pl.ds(me.owner * PLANE, PLANE)], vis1.at[pl.ds(0, PLANE)], own_sem.at[1]
     )
     vis_copy.start()
-    greet([me.on_plane(dy, dz)[1] for dy, dz in FAR_FIRST] + [me.near(i)[1] for i in range(1, NEAR)])
+    greet([me.on_plane(dy, dz)[1] for dy, dz in FAR_FIRST] + [me.near(i)[1] for i in range(1, NEAR)])()
 
     for dy, dz in FAR_FIRST:
         remote(start_ref, own_sky, sky_plane, 0, me.on_plane(dy, dz)[1]).start()
@@ -178,7 +182,7 @@
                 ],
                 axis=0,
             )
-            move = jnp.where(column == 4 * i + 2 * (source % 2) + j, 1.0, 0.0).astype(jnp.bfloat16)
+            move = jnp.where(column % GROUP == 4 * i + 2 * (source % 2) + j, 1.0, 0.0).astype(jnp.bfloat16)
             total += jnp.dot(spread.astype(jnp.bfloat16), move, preferred_element_type=jnp.float32)
     rows = 64.0 * total[:PLANE] + total[PLANE:]
     for d in range(PLANE):
@@ -258,40 +262,139 @@
     )(start_piece, strips, visibilities)
 
 
-def reduce_kernel(
-    final, step_size, g_ref, est_ref, out_ref, est_out, got1, sum1, got2, sum2, got3, sky, sems1, sems2, sems3, sems4, sems5, sems6
+def gather_rows(index_smem, sky_ref, strips, picked):
+    @pl.loop(0, OWNERS // 8)
+    def _(i):
+        block = sky_ref[pl.ds(i * 8, 8)].astype(jnp.float32)
+        strips[pl.ds(pl.multiple_of(i * 64, 64), 64)] = block.reshape(64, STRIP)
+
+    @pl.loop(0, PLANE)
+    def _(k):
+        for i in range(NEAR):
+            for q in range(4):
+                strip = index_smem[k, 0, 4 * i + q]
+                picked[q, k, pl.ds(i, 1)] = strips[pl.ds(strip, 1)]
+
+
+def back_projected(picked, vis_ref, kernel_ref, adjoint, adjoint_low):
+    for ch in range(2):
+        weights = kernel_ref[ch, 0]
+        gathered = jnp.concatenate(
+            [picked[2 * ch + j].reshape(BLOCKS, STRIP).astype(jnp.bfloat16) for j in range(TERMS)], axis=1
+        )
+        predicted = jnp.dot(gathered, weights, preferred_element_type=jnp.float32)
+        observed = vis_ref[ch].astype(jnp.float32)
+        residual = jnp.where(observed < FLAGGED, predicted - observed, 0.0).astype(jnp.bfloat16)
+        back = lax.dot_general(residual, weights, (((1,), (1,)), ((), ())), preferred_element_type=jnp.float32)
+        for j in range(TERMS):
+            adjoint[pl.ds(2 * ch + j, BLOCKS, stride=4)] = back[:, j * STRIP : (j + 1) * STRIP]
+
+    @pl.loop(0, READS // 128)
+    def _(i):
+        rows = pl.ds(pl.multiple_of(i * 128, 128), 128)
+        adjoint_low[rows] = adjoint[rows].astype(jnp.bfloat16)
+
+
+def selectors(index_ref, high_rows, low_hits):
+    group = lax.broadcasted_iota(jnp.int32, (1, STRIP), 1) // GROUP
+    row = lax.broadcasted_iota(jnp.int32, (HALF, STRIP), 0)
+    for m in range(READS // STRIP):
+        number = index_ref[4 * m]
+        for part in range(1, 4):
+            number = jnp.where(group == part, index_ref[4 * m + part], number)
+        high = number // HALF
+        high_rows[m] = jnp.broadcast_to(high, (16, STRIP))
+        low = jnp.broadcast_to(number - high * HALF, (HALF, STRIP))
+        low_hits[:, m * STRIP : (m + 1) * STRIP] = jnp.where(low == row, 1.0, 0.0).astype(jnp.bfloat16)
+
+
+def scatter_block(block, high_rows, low_hits, hits, adjoint_low):
+    for h in range(PLANE * PIECE // HALF):
+        for m in range(READS // STRIP):
+            lanes = slice(m * STRIP, (m + 1) * STRIP)
+            here = jnp.where(high_rows[m] == block * (PLANE * PIECE // HALF) + h, 1.0, 0.0).astype(jnp.bfloat16)
+            here = jnp.concatenate([here] * (HALF // 16), axis=0)
+            hits[h * HALF : (h + 1) * HALF, lanes] = here * low_hits[:, lanes]
+    return jnp.dot(hits[...], adjoint_low[...], preferred_element_type=jnp.float32)
+
+
+def iterate_kernel(
+    final,
+    step_size,
+    index_smem,
+    index_ref,
+    sky_ref,
+    vis_ref,
+    kernel_ref,
+    est_ref,
+    out_ref,
+    est_out,
+    strips,
+    picked,
+    adjoint,
+    adjoint_low,
+    high_rows,
+    low_hits,
+    hits,
+    image,
+    got1,
+    sum1,
+    got2,
+    sum2,
+    got3,
+    sky,
+    sems1,
+    sems2,
+    sems3,
+    sems4,
+    sems5,
+    sems6,
 ):
     me = Place()
     targets = [me.on_plane(dy, dz)[1] for dy, dz in FAR_FIRST]
     if final:
         targets += [me.on_chan(dy, dx) for dy, dx in CHAN_FAR_FIRST if dy and dx]
-    greet(targets + [me.on_x(dx) for dx in (2, 1, 3)] + [me.partner])
-
-    order = [1, 3, 2, 0]
+    wait_for_all = greet(targets + [me.on_x(dx) for dx in (2, 1, 3)] + [me.partner])
 
     def own_block(xx):
         return pl.ds((me.core * NX + xx) * PLANE, PLANE)
 
     def pair_copy(dx):
-        block = g_ref.at[pl.ds(((1 - me.core) * NX + me.xs[dx]) * PLANE, PLANE)]
+        block = image.at[pl.ds(((1 - me.core) * NX + lax.rem(me.x + dx, NX)) * PLANE, PLANE)]
         return remote(block, got1.at[dx], sems1, dx, me.partner)
 
-    for dx in order:
-        pair_copy(dx).start()
-
     def x_copy(dx):
-        return remote(sum1.at[dx], got2.at[dx], sems2, dx, me.on_x(dx))
-
-    for dx in order[:-1]:
-        pair_copy(dx).wait_recv()
-        base = (me.core * NX + me.xs[dx]) * PLANE
-
-        @pl.loop(0, PLANE // 8)
-        def _(i):
-            total = g_ref[pl.ds(base + i * 8, 8)].astype(jnp.float32) + got1[dx, pl.ds(i * 8, 8)].astype(jnp.float32)
-            sum1[dx, pl.ds(i * 8, 8)] = total.astype(jnp.bfloat16)
-
-        x_copy(dx).start()
+        target = (me.y * NX + lax.rem(me.x + dx, NX), me.facet)
+        return remote(sum1.at[dx], got2.at[dx], sems2, dx, target)
+
+    gather_rows(index_smem, sky_ref, strips, picked)
+    back_projected(picked, vis_ref, kernel_ref, adjoint, adjoint_low)
+    selectors(index_ref, high_rows, low_hits)
+
+    @pl.loop(0, 2 * NX)
+    def _(t):
+        dx = lax.rem(t + 1, NX)
+        core = jnp.where(t < NX, 1 - me.core, me.core)
+        block = core * NX + lax.rem(me.x + dx, NX)
+        part = scatter_block(block, high_rows, low_hits, hits, adjoint_low)
+        image[pl.ds(block * PLANE, PLANE)] = part.reshape(PLANE, PIECE, STRIP).astype(jnp.bfloat16)
+
+        @pl.when(t == NX - 1)
+        def _():
+            wait_for_all()
+            for first in (1, 2, 3, 0):
+                pair_copy(first).start()
+
+        @pl.when(jnp.logical_and(t >= NX, t < 2 * NX - 1))
+        def _():
+            pair_copy(dx).wait_recv()
+            for i in range(PLANE // 8):
+                mine = image[pl.ds(block * PLANE + i * 8, 8)].astype(jnp.float32)
+                total = mine + got1[dx, pl.ds(i * 8, 8)].astype(jnp.float32)
+                sum1[dx, pl.ds(i * 8, 8)] = total.astype(jnp.bfloat16)
+            x_copy(dx).start()
+
+    order = [1, 2, 3, 0]
     pair_copy(0).wait_recv()
     for dx in order[:-1]:
         x_copy(dx).wait_recv()
@@ -300,7 +403,7 @@
     @pl.loop(0, PLANE // 8)
     def _(i):
         rows = pl.ds(i * 8, 8)
-        total = g_ref[pl.ds(base + i * 8, 8)].astype(jnp.float32) + got1[0, rows].astype(jnp.float32)
+        total = image[pl.ds(base + i * 8, 8)].astype(jnp.float32) + got1[0, rows].astype(jnp.float32)
         for dx in order[:-1]:
             total += got2[dx, rows].astype(jnp.float32)
         sum2[rows] = total.astype(jnp.bfloat16)
@@ -366,28 +469,38 @@
     all_plane.wait_send()
 
 
-def reduce_step(final, step_size, gradient, estimate):
+def iterate(final, step_size, index, sky_now, visibilities, kernels, estimate):
     def body(*refs):
-        reduce_kernel(final, step_size, *refs)
+        iterate_kernel(final, step_size, *refs)
 
     dma = pltpu.SemaphoreType.DMA
+    vmem = pltpu.VMEM
+    blocks = (NX, PLANE, PIECE, STRIP)
     if final:
         out = jax.ShapeDtypeStruct((2 * NY * NX, 4 * STRIP), jnp.float32)
-        sky = pltpu.VMEM((NY * NX * PIECE, STRIP), jnp.float32)
+        sky = vmem((NY * NX * PIECE, STRIP), jnp.float32)
     else:
-        sky = pltpu.VMEM((OWNERS, PIECE, STRIP), jnp.bfloat16)
         out = jax.ShapeDtypeStruct((OWNERS, PIECE, STRIP), jnp.bfloat16)
+        sky = vmem(out.shape, out.dtype)
     return pl.pallas_call(
         body,
         out_shape=(out, jax.ShapeDtypeStruct((PIECE, STRIP), jnp.float32)),
-        in_specs=[pl.BlockSpec(memory_space=pltpu.VMEM)] * 2,
-        out_specs=(pl.BlockSpec(memory_space=pltpu.VMEM),) * 2,
+        in_specs=[pl.BlockSpec(memory_space=pltpu.SMEM)] + [pl.BlockSpec(memory_space=vmem)] * 5,
+        out_specs=(pl.BlockSpec(memory_space=vmem),) * 2,
         scratch_shapes=[
-            pltpu.VMEM((NX, PLANE, PIECE, STRIP), jnp.bfloat16),
-            pltpu.VMEM((NX, PLANE, PIECE, STRIP), jnp.bfloat16),
-            pltpu.VMEM((NX, PLANE, PIECE, STRIP), jnp.bfloat16),
-            pltpu.VMEM((PLANE, PIECE, STRIP), jnp.bfloat16),
-            pltpu.VMEM((PLANE, PIECE, STRIP), jnp.bfloat16),
+            vmem((OWNERS * PIECE, STRIP), jnp.float32),
+            vmem((4, PLANE, NEAR, STRIP), jnp.float32),
+            vmem((READS, STRIP), jnp.float32),
+            vmem((READS, STRIP), jnp.bfloat16),
+            vmem((READS // STRIP, 16, STRIP), jnp.int32),
+            vmem((HALF, READS), jnp.bfloat16),
+            vmem((PLANE * PIECE, READS), jnp.bfloat16),
+            vmem((OWNERS, PIECE, STRIP), jnp.bfloat16),
+            vmem(blocks, jnp.bfloat16),
+            vmem(blocks, jnp.bfloat16),
+            vmem(blocks, jnp.bfloat16),
+            vmem(blocks[1:], jnp.bfloat16),
+            vmem(blocks[1:], jnp.bfloat16),
             sky,
             dma((2, NX)),
             dma((2, NX)),
@@ -397,70 +510,8 @@
             dma((2, NX)),
         ],
         compiler_params=pltpu.CompilerParams(collective_id=1 if final else 0, has_side_effects=True),
-        name="reduce_final" if final else "reduce_sky",
-    )(gradient, estimate)
-
-
-def gradient_kernel(index_ref, sky_ref, vis_ref, kernel_ref, out_ref, strips, picked, adjoint, *sums):
-    @pl.loop(0, OWNERS // 8)
-    def _(i):
-        block = sky_ref[pl.ds(i * 8, 8)].astype(jnp.float32)
-        strips[pl.ds(pl.multiple_of(i * 64, 64), 64)] = block.reshape(64, STRIP)
-        for total in sums:
-            total[pl.ds(pl.multiple_of(i * 64, 64), 64)] = jnp.zeros((64, STRIP), jnp.float32)
-
-    @pl.loop(0, PLANE)
-    def _(k):
-        for i in range(NEAR):
-            for q in range(4):
-                strip = index_ref[k, 0, 4 * i + q]
-                picked[q, k, pl.ds(i, 1)] = strips[pl.ds(strip, 1)]
-
-    for ch in range(2):
-        weights = kernel_ref[ch, 0]
-        gathered = jnp.concatenate(
-            [picked[2 * ch + j].reshape(PLANE * NEAR, STRIP).astype(jnp.bfloat16) for j in range(TERMS)], axis=1
-        )
-        predicted = jnp.dot(gathered, weights, preferred_element_type=jnp.float32)
-        observed = vis_ref[ch].astype(jnp.float32)
-        residual = jnp.where(observed < FLAGGED, predicted - observed, 0.0).astype(jnp.bfloat16)
-        back = lax.dot_general(residual, weights, (((1,), (1,)), ((), ())), preferred_element_type=jnp.float32)
-        for j in range(TERMS):
-            adjoint[2 * ch + j] = back[:, j * STRIP : (j + 1) * STRIP].reshape(PLANE, NEAR, STRIP)
-
-    @pl.loop(0, PLANE)
-    def _(k):
-        for i in range(NEAR):
-            for q in range(4):
-                total = sums[(4 * i + q) % len(sums)]
-                strip = index_ref[k, 0, 4 * i + q]
-                total[pl.ds(strip, 1)] += adjoint[q, k, pl.ds(i, 1)]
-
-    @pl.loop(0, OWNERS // 8)
-    def _(i):
-        rows = pl.ds(pl.multiple_of(i * 64, 64), 64)
-        block = sums[0][rows]
-        for total in sums[1:]:
-            block += total[rows]
-        out_ref[pl.ds(i * 8, 8)] = block.reshape(8, 8, STRIP).astype(jnp.bfloat16)
-
-
-SUMS = 8
-
-
-def gradient_step(index, sky, visibilities, kernels):
-    vmem = pltpu.VMEM
-    image = (OWNERS * PIECE, STRIP)
-    rows = (4, PLANE, NEAR, STRIP)
-    return pl.pallas_call(
-        gradient_kernel,
-        out_shape=jax.ShapeDtypeStruct((OWNERS, PIECE, STRIP), jnp.bfloat16),
-        in_specs=[pl.BlockSpec(memory_space=pltpu.SMEM)] + [pl.BlockSpec(memory_space=vmem)] * 3,
-        out_specs=pl.BlockSpec(memory_space=vmem),
-        scratch_shapes=[vmem(image, jnp.float32), vmem(rows, jnp.float32), vmem(rows, jnp.float32)]
-        + [vmem(image, jnp.float32)] * SUMS,
-        name="gradient",
-    )(index, sky, visibilities, kernels)
+        name="iterate_final" if final else "iterate_sky",
+    )(index, index, sky_now, visibilities, kernels, estimate)
 
 
 def owner_order(strip):
@@ -495,8 +546,7 @@
     )
     observed = observed.reshape(slot_count, 2, 2 * VISB).swapaxes(0, 1)
     for iteration in range(ITERS):
-        gradient = gradient_step(picked, sky, observed, uv_kernels)
-        sky, estimate = reduce_step(iteration == ITERS - 1, step_size, gradient, estimate)
+        sky, estimate = iterate(iteration == ITERS - 1, step_size, picked, sky, observed, uv_kernels, estimate)
     return sky
 
 

time: 140 us -> 125 us (0.89)
  Pallas kernels: 129 us -> 115 us
    pallas_call x4 -> x2, Pallas kernels: 89.2 us -> 74.4 us  [iterate(): pl.pallas_call(body, out_shape=(out, jax.ShapeDtypeStruct((PIECE, STRIP),...]
where the time goes in v5:
time: 125 us; the launch traced here: 124 us
  Pallas kernels  115 us (92%)
  local copies, waits for them, and re-layouts  7.41 us (6%)
  other arithmetic  2.11 us (2%)
    pallas_call x2, Pallas kernels, iterate(): pl.pallas_call(body, out_shape=(out, jax.ShapeDtypeStruct((PIECE, STRIP),...  74.4 us
    pallas_call x1, Pallas kernels, exchange(): pl.pallas_call(exchange_kernel, out_shape=(jax.ShapeDtypeStruct(sky, jnp....  40.3 us
    reshape x2, local copies, waits for them, and re-layouts, on_device(): observed = observed.reshape(slot_count, 2, 2 * VISB).swapaxes(0, 1)  2.78 us
    unnamed x9, local copies, waits for them, and re-layouts  2.55 us

profile of v5, /device:TPU:1, one launch (start us, length us, event | category | flops | bytes accessed | tf_op | source)
XLA Modules:
  0.0 124.2 jit_solution(13867012012677659443)
XLA Ops:
  0.0 0.0 copy-start
  0.0 0.0 copy-start.2
  0.0 0.9 copy-done
  0.9 0.0 copy-start.1
  0.9 0.6 convert_element_type.3.start_ref
  1.5 0.0 copy-done.2
  1.5 0.3 fusion.5
  1.8 0.0 copy-done.1
  1.8 0.0 copy-start.3
  1.8 0.6 pad.4.meta_ref
  2.4 0.1 copy-done.3
  2.5 0.1 copy.8
  2.6 1.2 %compare_select_fusion = bf16[1,64,16,256]{3,2,1,0:T(8,128)(2,1)S(1)} fusion(bf16[1,64,16,256]{3,2,1,0:T(8,128)(2,1)} %param.6, s32[64,16]{1,0:T(8,128)S(1)} %copy.8, s32[256]{0:T(256)S(1)} %and_select_fusion.10), kind=kLoop, calls=%fused_computation | loop fusion | flops 524288 | bytes 1053696 | tf_op jit(solution)/shard_map/jit(_where)/select_n | solution.py:536
  3.8 0.1 reshape.35
  4.0 1.2 copy.9
  5.2 40.3 %exchange.1 = (bf16[512,8,128]{2,1,0:T(8,128)(2,1)}, s32[64,1,128]{2,1,0:T(1,128)}, bf16[64,8,4,128]{3,2,1,0:T(4,128)(2,1)}) custom-call(bf16[8,128]{1,0:T(8,128)(2,1)} %convert_element_type.3.start_ref, s32[32,128]{1,0:T(8,128)} %pad.4.meta_ref, bf16[512,4,128]{2,1,0:T(4,128)(2,1)} %bitcast.14), custom_call_target="tpu_custom_call" | custom-call | tf_op jit(solution)/shard_map/exchange/pallas_call | solution.py:235
  45.5 1.9 %reshape.37 = bf16[512,2,256]{2,1,0:T(2,128)(2,1)S(1)} reshape(bf16[64,8,4,128]{3,2,1,0:T(4,128)(2,1)} %get-tuple-element.13) | data formatting | bytes 1048576 | tf_op jit(solution)/shard_map/reshape | solution.py:547
  47.4 0.9 copy.12
  48.3 43.3 %iterate_sky.1 = (bf16[512,8,128]{2,1,0:T(8,128)(2,1)}, f32[8,128]{1,0:T(8,128)}) custom-call(s32[64,1,128]{2,1,0:T(1,128)} %get-tuple-element.11.refs_0_.refs_1_, s32[64,1,128]{2,1,0:T(1,128)} %get-tuple-element.11.refs_0_.refs_1_, bf16[512,8,128]{2,1,0:T(8,128)(2,1)} %get-tuple-element.12.refs_2_, bf16[2,512,256]{2,1,0:T(8,128)(2,1)} %bitcast.12, ...), custom_call_target="tpu_custom_call" | custom-call | tf_op jit(solution)/shard_map/iterate_sky/pallas_call | solution.py:485
  91.6 31.1 %iterate_final.1 = (f32[64,512]{1,0:T(8,128)}, f32[8,128]{1,0:T(8,128)}) custom-call(s32[64,1,128]{2,1,0:T(1,128)} %get-tuple-element.11.refs_0_.refs_1_, s32[64,1,128]{2,1,0:T(1,128)} %get-tuple-element.11.refs_0_.refs_1_, bf16[512,8,128]{2,1,0:T(8,128)(2,1)} %get-tuple-element.14.refs_2_, bf16[2,512,256]{2,1,0:T(8,128)(2,1)} %bitcast.13, ...), custom_call_target="tpu_custom_call" | custom-call | tf_op jit(solution)/shard_map/iterate_final/pallas_call | solution.py:485
  122.7 1.6 %copy.14 = f32[64,512]{1,0:T(8,128)} copy(f32[64,512]{1,0:T(8,128)} %get-tuple-element.16) | data formatting | bytes 262144
  (3 shorter events, 0.0 us)
Async XLA Ops:
  0.0 0.9 copy-start
  0.0 1.5 %copy-start.2 = (s32[1,64,16,2]{1,3,2,0:T(2,128)S(1)}, s32[1,64,16,2]{1,3,2,0:T(2,128)}, u32[]{:S(2)}) copy-start(s32[1,64,16,2]{1,3,2,0:T(2,128)} %param.7) | copy-start | bytes 24580
  0.9 0.9 copy-start.1
  1.8 0.7 copy-start.3

commit v6 on v0

v6 whole, which is shorter than its diff:
```python
import jax
import jax.numpy as jnp
from jax import lax
from jax.experimental import pallas as pl
from jax.experimental.pallas import tpu as pltpu
from jax.sharding import PartitionSpec as P

STRIP = 128
VISB = 128
TERMS = 2
ITERS = 2
NX = 4
NY = 8
NZ = 8
PLANE = NY * NZ
OWNERS = 2 * NX * PLANE
PIECE = 8
NEAR = 2 * NX
GROUP = 4 * NEAR
BLOCKS = PLANE * NEAR
READS = 4 * BLOCKS
HALF = 64

FLAGGED = 1024.0

shrinkage = 0.05
MESH = pl.DeviceIdType.MESH


class Place:
    def __init__(self):
        chan = lax.axis_index("chan")
        facet = lax.axis_index("facet")
        self.chan, self.facet = chan, facet
        self.y, self.x = chan // NX, chan % NX
        self.z, self.core = facet // 2, facet % 2
        self.spot = self.y * NZ + self.z
        self.owner = self.core * NX + self.x
        self.ys = [lax.rem(self.y + d, NY) for d in range(NY)]
        self.zs = [lax.rem(self.z + d, NZ) for d in range(NZ)]
        self.xs = [lax.rem(self.x + d, NX) for d in range(NX)]
        self.chan_y = [yy * NX + self.x for yy in self.ys]
        self.facet_z = [zz * 2 + self.core for zz in self.zs]
        self.partner = (chan, self.z * 2 + (1 - self.core))

    def on_x(self, dx):
        return (self.y * NX + self.xs[dx], self.facet)

    def on_plane(self, dy, dz):
        return self.ys[dy] * NZ + self.zs[dz], (self.chan_y[dy], self.facet_z[dz])

    def on_chan(self, dy, dx):
        return (self.ys[dy] * NX + self.xs[dx], self.facet)

    def near(self, i):
        core = lax.rem(self.core + lax.rem(i, 2), 2)
        step = i // 2
        xx = lax.rem(self.x + step * (step + 1) // 2, NX)
        return core * NX + xx, (self.y * NX + xx, self.z * 2 + core)


def reach(d, length):
    return min(d, length - d)


FAR_FIRST = sorted(
    ((dy, dz) for dy in range(NY) for dz in range(NZ) if dy or dz),
    key=lambda step: -reach(step[0], NY) - reach(step[1], NZ),
)
CHAN_FAR_FIRST = sorted(
    ((dy, dx) for dy in range(NY) for dx in range(NX) if dy or dx),
    key=lambda step: -reach(step[0], NY) - reach(step[1], NX),
)


def remote(src, dst, sems, at, target):
    return pltpu.make_async_remote_copy(
        src_ref=src,
        dst_ref=dst,
        send_sem=sems.at[0, at],
        recv_sem=sems.at[1, at],
        device_id=target,
        device_id_type=MESH,
    )


def greet(targets):
    barrier = pltpu.get_barrier_semaphore()
    for target in targets:
        pl.semaphore_signal(barrier, inc=1, device_id=target, device_id_type=MESH)
    return lambda: pl.semaphore_wait(barrier, len(targets))


def owner_order(strip):
    quarter = strip % 4
    core = strip // 4 % 2
    z = strip // 8 % 8
    low_row = strip // 64 % 2
    x = strip // 128 % 4
    y = strip // 512
    return (((core * NX + x) * NY + y) * NZ + z) * PIECE + low_row * 4 + quarter


def gather_rows(index_smem, sky_ref, strips, picked):
    @pl.loop(0, OWNERS // 8)
    def _(i):
        block = sky_ref[pl.ds(i * 8, 8)].astype(jnp.float32)
        strips[pl.ds(pl.multiple_of(i * 64, 64), 64)] = block.reshape(64, STRIP)

    @pl.loop(0, PLANE)
    def _(k):
        for i in range(NEAR):
            for q in range(4):
                strip = index_smem[k, 0, 4 * i + q]
                picked[q, k, pl.ds(i, 1)] = strips[pl.ds(strip, 1)]


def selectors(index_ref, high_rows, low_hits):
    group = lax.broadcasted_iota(jnp.int32, (1, STRIP), 1) // GROUP
    row = lax.broadcasted_iota(jnp.int32, (HALF, STRIP), 0)
    for m in range(READS // STRIP):
        number = index_ref[4 * m]
        for part in range(1, 4):
            number = jnp.where(group == part, index_ref[4 * m + part], number)
        high = number // HALF
        high_rows[m] = jnp.broadcast_to(high, (16, STRIP))
        low = jnp.broadcast_to(number - high * HALF, (HALF, STRIP))
        low_hits[:, m * STRIP : (m + 1) * STRIP] = jnp.where(low == row, 1.0, 0.0).astype(jnp.bfloat16)


def scatter_block(block, high_rows, low_hits, hits, adjoint_low):
    for h in range(PLANE * PIECE // HALF):
        for m in range(READS // STRIP):
            lanes = slice(m * STRIP, (m + 1) * STRIP)
            here = jnp.where(high_rows[m] == block * (PLANE * PIECE // HALF) + h, 1.0, 0.0).astype(jnp.bfloat16)
            here = jnp.concatenate([here] * (HALF // 16), axis=0)
            hits[h * HALF : (h + 1) * HALF, lanes] = here * low_hits[:, lanes]
    return jnp.dot(hits[...], adjoint_low[...], preferred_element_type=jnp.float32)


class Named:
    def __init__(self, names, refs):
        for name, ref in zip(names, refs):
            setattr(self, name, ref)


def scratch_shapes():
    vmem = pltpu.VMEM
    dma = pltpu.SemaphoreType.DMA
    low, wide, whole = jnp.bfloat16, jnp.float32, jnp.int32
    blocks = (NX, PLANE, PIECE, STRIP)
    index = (PLANE, 1, STRIP)
    shapes = dict(
        estimate=vmem((PIECE, STRIP), wide),
        start=vmem((PIECE, STRIP), low),
        numbers=vmem((NZ * 4, STRIP), whole),
        near_numbers=vmem((NEAR, NZ * 4, STRIP), whole),
        packed=vmem(index, wide),
        index_in=vmem(index, wide),
        index_now=vmem(index, whole),
        index_smem=pltpu.SMEM(index, whole),
        mixed=vmem((4 * 2 * NZ, STRIP), wide),
        vis_send=vmem((OWNERS, 4, STRIP), low),
        vis_near=vmem((NEAR * PLANE, 4, STRIP), low),
        vis_in=vmem((PLANE, NEAR, 4, STRIP), low),
        observed=vmem((READS, STRIP), wide),
        strips=vmem((OWNERS * PIECE, STRIP), wide),
        picked=vmem((4, PLANE, NEAR, STRIP), wide),
        adjoint=vmem((READS, STRIP), wide),
        adjoint_low=vmem((READS, STRIP), low),
        high_rows=vmem((READS // STRIP, 16, STRIP), whole),
        low_hits=vmem((HALF, READS), low),
        hits=vmem((PLANE * PIECE, READS), low),
        image=vmem((OWNERS, PIECE, STRIP), low),
        final_image=vmem((NY * NX * PIECE, STRIP), wide),
        to_chan=dma((2, 1)),
        to_meta_near=dma((2, NEAR)),
        to_meta_plane=dma((2, 1)),
        to_vis_near=dma((2, NEAR)),
        to_vis_plane=dma((2, 1)),
        local=dma((2,)),
    )
    for it in range(ITERS):
        shapes.update(
            {
                f"sky{it}": vmem((OWNERS, PIECE, STRIP), low),
                f"to_sky_plane{it}": dma((2, 1)),
                f"to_sky_x{it}": dma((2, NX)),
                f"to_sky_pair{it}": dma((2, NX)),
                f"got_pair{it}": vmem(blocks, low),
                f"sum_pair{it}": vmem(blocks, low),
                f"got_x{it}": vmem(blocks, low),
                f"sum_x{it}": vmem(blocks[1:], low),
                f"got_plane{it}": vmem(blocks[1:], low),
                f"to_pair{it}": dma((2, NX)),
                f"to_x{it}": dma((2, NX)),
                f"to_plane{it}": dma((2, 1)),
            }
        )
    return shapes


def of_iteration(s, it):
    names = [name[:-1] for name in vars(s) if name.endswith(str(it))]
    return Named(names, [getattr(s, name + str(it)) for name in names])


def prepare(me, s, start_ref, index_ref, counts_ref, vis_ref):
    for quarter in range(4):
        columns = slice(quarter * STRIP, (quarter + 1) * STRIP)
        s.mixed[:8] = start_ref[pl.ds(pl.multiple_of(me.chan // 4 * 8, 8), 8), columns]
        for low in range(2):
            s.estimate[4 * low + quarter : 4 * low + quarter + 1] = s.mixed[pl.ds(me.chan % 4 * 2 + low, 1)]
    s.start[...] = s.estimate[...].astype(jnp.bfloat16)
    s.sky0[me.owner * PLANE + me.spot] = s.estimate[...].astype(jnp.bfloat16)
    channels = index_ref.shape[1]
    s.numbers[...] = jnp.zeros(s.numbers.shape, jnp.int32)
    s.numbers[:, :channels] = owner_order(index_ref[...])
    lane = lax.broadcasted_iota(jnp.int32, (2 * NZ, STRIP), 1)
    for y in range(NY):
        for x in range(NX):
            for ch in range(2):
                chan = (y * NX + x) * 2 + ch
                live = lane < counts_ref[:, chan : chan + 1]
                for half in range(2):
                    block = vis_ref[chan, :, half * STRIP : (half + 1) * STRIP].astype(jnp.float32)
                    s.mixed[pl.ds(ch * 2 + half, 2 * NZ, stride=4)] = jnp.where(live, block, FLAGGED)
            for z in range(NZ):
                for core in range(2):
                    row = (z * 2 + core) * 4
                    owner = ((core * NX + x) * NY + y) * NZ + z
                    s.vis_send[owner] = s.mixed[row : row + 4].astype(jnp.bfloat16)


def spread_sky_plane(me, sky, sems, source):
    own = sky.at[me.owner * PLANE + me.spot]
    for dy, dz in FAR_FIRST:
        remote(own if source is None else source, own, sems, 0, me.on_plane(dy, dz)[1]).start()
    others = sky.at[pl.ds(0, PLANE - 1)]
    return remote(others, others, sems, 0, me.partner)


def sky_spreaders(me, t):
    def own_block(dx):
        return t.sky.at[pl.ds((me.core * NX + me.xs[dx]) * PLANE, PLANE)]

    def spread_x(dx):
        return remote(own_block(0), own_block(0), t.to_sky_x, dx, me.on_x(dx))

    def spread_pair(dx):
        return remote(own_block(dx), own_block(dx), t.to_sky_pair, dx, me.partner)

    return spread_x, spread_pair


def pack_numbers(me, s):
    lane = lax.broadcasted_iota(jnp.int32, (PLANE, STRIP), 1)
    place = lax.broadcasted_iota(jnp.int32, (PLANE, STRIP), 0)
    belongs = (lane // 2) == (place // NZ) * NX + me.x
    column = lax.broadcasted_iota(jnp.int32, (STRIP, STRIP), 1)
    source = lax.broadcasted_iota(jnp.int32, (STRIP, STRIP), 0)
    total = jnp.zeros((2 * PLANE, STRIP), jnp.float32)
    for i in range(NEAR):
        held = s.numbers if i == 0 else s.near_numbers.at[i]
        for j in range(TERMS):
            strips = held[pl.ds(me.core * 2 + j, NZ, stride=4)]
            high = strips // 64
            low = strips - 64 * high
            spread = jnp.concatenate(
                [
                    jnp.where(belongs, jnp.concatenate([part.astype(jnp.float32)] * NY, axis=0), 0.0)
                    for part in (high, low)
                ],
                axis=0,
            )
            move = jnp.where(column % GROUP == 4 * i + 2 * (source % 2) + j, 1.0, 0.0).astype(jnp.bfloat16)
            total += jnp.dot(spread.astype(jnp.bfloat16), move, preferred_element_type=jnp.float32)
    rows = 64.0 * total[:PLANE] + total[PLANE:]
    for d in range(PLANE):
        s.packed[d] = rows[d : d + 1]
    s.index_in[0] = s.packed[me.spot]


def exchange(me, s):
    t = of_iteration(s, 0)
    own_vis = pltpu.make_async_copy(
        s.vis_send.at[pl.ds(me.owner * PLANE, PLANE)], s.vis_near.at[pl.ds(0, PLANE)], s.local.at[0]
    )
    own_vis.start()
    all_sky = spread_sky_plane(me, t.sky, t.to_sky_plane, s.start)
    spread_x, spread_pair = sky_spreaders(me, t)

    def near_meta(i):
        return remote(s.numbers, s.near_numbers.at[i], s.to_meta_near, i, me.near(i)[1])

    def near_vis(i):
        owner, target = me.near(i)
        block = s.vis_send.at[pl.ds(owner * PLANE, PLANE)]
        return remote(block, s.vis_near.at[pl.ds(i * PLANE, PLANE)], s.to_vis_near, i, target)

    for i in range(1, NEAR):
        near_meta(i).start()
    for i in range(1, NEAR):
        near_vis(i).start()
    own_vis.wait()

    def forward(i):
        base = i * PLANE
        s.vis_in[0, i] = s.vis_near[base + me.spot]
        for dy, dz in FAR_FIRST:
            place, target = me.on_plane(dy, dz)
            remote(s.vis_near.at[base + place], s.vis_in.at[dy * NZ + dz, i], s.to_vis_plane, 0, target).start()

    forward(0)
    for i in range(1, NEAR):
        near_meta(i).wait_recv()
    pack_numbers(me, s)
    for dy, dz in FAR_FIRST:
        spot, target = me.on_plane(dy, dz)
        remote(s.packed.at[spot], s.index_in.at[dy * NZ + dz], s.to_meta_plane, 0, target).start()
    near_vis(1).wait_recv()
    forward(1)
    all_sky.wait_recv()
    for dx in (2, 1, 3):
        spread_x(dx).start()
    spread_pair(0).start()

    @pl.loop(2, NEAR)
    def _(i):
        near_vis(i).wait_recv()
        forward(i)

    far_index = s.index_in.at[pl.ds(1, PLANE - 1)]
    all_index = remote(far_index, far_index, s.to_meta_plane, 0, me.partner)
    all_index.wait_recv()
    s.index_now[...] = jnp.clip(s.index_in[...].astype(jnp.int32), 0, OWNERS * PIECE - 1)
    to_smem = pltpu.make_async_copy(s.index_now, s.index_smem, s.local.at[1])
    to_smem.start()
    selectors(s.index_now, s.high_rows, s.low_hits)
    for dx in (1, 3, 2):
        spread_x(dx).wait_recv()
        spread_pair(NX - dx).start()
    to_smem.wait()
    for dx in range(NX):
        spread_pair(dx).wait_recv()
    gather_rows(s.index_smem, t.sky, s.strips, s.picked)

    arrived = s.vis_in.at[pl.ds(1, PLANE - 1)]
    all_vis = remote(arrived, arrived, s.to_vis_plane, 0, me.partner)
    all_vis.wait_recv()

    @pl.loop(0, PLANE)
    def _(k):
        rows = pl.ds(pl.multiple_of(k * 4 * NEAR, 4 * NEAR), 4 * NEAR)
        s.observed[rows] = s.vis_in[k].astype(jnp.float32).reshape(4 * NEAR, STRIP)

    def finish():
        all_index.wait_send()
        all_vis.wait_send()
        all_sky.wait_send()
        for dx in range(1, NX):
            spread_x(dx).wait_send()
        for dx in range(NX):
            spread_pair(dx).wait_send()
        for i in range(1, NEAR):
            near_meta(i).wait_send()
            near_vis(i).wait_send()

    return finish


def back_projected(s, kernel_ref):
    for ch in range(2):
        weights = kernel_ref[ch, 0]
        gathered = jnp.concatenate(
            [s.picked[2 * ch + j].reshape(BLOCKS, STRIP).astype(jnp.bfloat16) for j in range(TERMS)], axis=1
        )
        predicted = jnp.dot(gathered, weights, preferred_element_type=jnp.float32)
        halves = []
        for half in range(2):
            observed = s.observed[pl.ds(2 * ch + half, BLOCKS, stride=4)]
            model = predicted[:, half * STRIP : (half + 1) * STRIP]
            halves.append(jnp.where(observed < FLAGGED, model - observed, 0.0).astype(jnp.bfloat16))
        residual = jnp.concatenate(halves, axis=1)
        back = lax.dot_general(residual, weights, (((1,), (1,)), ((), ())), preferred_element_type=jnp.float32)
        for j in range(TERMS):
            s.adjoint[pl.ds(2 * ch + j, BLOCKS, stride=4)] = back[:, j * STRIP : (j + 1) * STRIP]

    @pl.loop(0, READS // 128)
    def _(i):
        rows = pl.ds(pl.multiple_of(i * 128, 128), 128)
        s.adjoint_low[rows] = s.adjoint[rows].astype(jnp.bfloat16)


def reduce_gradient(me, s, it):
    t = of_iteration(s, it)

    def pair_copy(dx):
        block = s.image.at[pl.ds(((1 - me.core) * NX + lax.rem(me.x + dx, NX)) * PLANE, PLANE)]
        return remote(block, t.got_pair.at[dx], t.to_pair, dx, me.partner)

    def x_copy(dx):
        target = (me.y * NX + lax.rem(me.x + dx, NX), me.facet)
        return remote(t.sum_pair.at[dx], t.got_x.at[dx], t.to_x, dx, target)

    @pl.loop(0, 2 * NX)
    def _(step):
        dx = lax.rem(step + 1, NX)
        core = jnp.where(step < NX, 1 - me.core, me.core)
        block = core * NX + lax.rem(me.x + dx, NX)
        part = scatter_block(block, s.high_rows, s.low_hits, s.hits, s.adjoint_low)
        s.image[pl.ds(block * PLANE, PLANE)] = part.reshape(PLANE, PIECE, STRIP).astype(jnp.bfloat16)

        @pl.when(step < NX)
        def _():
            pair_copy(dx).start()

        @pl.when(jnp.logical_and(step >= NX, step < 2 * NX - 1))
        def _():
            pair_copy(dx).wait_recv()
            for i in range(PLANE // 8):
                mine = s.image[pl.ds(block * PLANE + i * 8, 8)].astype(jnp.float32)
                total = mine + t.got_pair[dx, pl.ds(i * 8, 8)].astype(jnp.float32)
                t.sum_pair[dx, pl.ds(i * 8, 8)] = total.astype(jnp.bfloat16)
            x_copy(dx).start()

    pair_copy(0).wait_recv()
    for dx in range(1, NX):
        x_copy(dx).wait_recv()

    @pl.loop(0, PLANE // 8)
    def _(i):
        rows = pl.ds(i * 8, 8)
        total = s.image[pl.ds(me.owner * PLANE + i * 8, 8)].astype(jnp.float32) + t.got_pair[0, rows].astype(jnp.float32)
        for dx in range(1, NX):
            total += t.got_x[dx, rows].astype(jnp.float32)
        t.sum_x[rows] = total.astype(jnp.bfloat16)

    for dy, dz in FAR_FIRST:
        place, target = me.on_plane(dy, dz)
        remote(t.sum_x.at[place], t.got_plane.at[dy * NZ + dz], t.to_plane, 0, target).start()
    others = t.got_plane.at[pl.ds(1, PLANE - 1)]
    all_plane = remote(others, others, t.to_plane, 0, me.partner)
    all_plane.wait_recv()
    parts = [t.sum_x[me.spot].astype(jnp.float32)] + [jnp.zeros((PIECE, STRIP), jnp.float32) for _ in range(3)]
    for k in range(1, PLANE):
        parts[k % 4] += t.got_plane[k].astype(jnp.float32)

    def finish():
        for dx in range(NX):
            pair_copy(dx).wait_send()
        for dx in range(1, NX):
            x_copy(dx).wait_send()
        all_plane.wait_send()

    return (parts[0] + parts[1]) + (parts[2] + parts[3]), finish


def reconstruct_kernel(step_size, names, start_ref, index_ref, counts_ref, vis_ref, kernel_ref, out_ref, *scratch):
    s = Named(names, scratch)
    me = Place()
    wait_for_all = greet(
        [me.on_plane(dy, dz)[1] for dy, dz in FAR_FIRST]
        + [me.on_chan(dy, dx) for dy, dx in CHAN_FAR_FIRST if dy and dx]
        + [me.near(i)[1] for i in range(1, NEAR)]
    )
    prepare(me, s, start_ref, index_ref, counts_ref, vis_ref)
    wait_for_all()
    waits = [exchange(me, s)]
    for it in range(ITERS):
        if it:
            gather_rows(s.index_smem, getattr(s, f"sky{it}"), s.strips, s.picked)
        back_projected(s, kernel_ref)
        gradient, finish = reduce_gradient(me, s, it)
        estimate = jnp.maximum(s.estimate[...] - step_size * gradient - shrinkage, 0.0)
        if it == ITERS - 1:
            mine = s.final_image.at[pl.ds(pl.multiple_of(me.chan * PIECE, PIECE), PIECE)]
            mine[...] = estimate
            for dy, dx in CHAN_FAR_FIRST:
                remote(mine, mine, s.to_chan, 0, me.on_chan(dy, dx)).start()
            rest = s.final_image.at[pl.ds(0, (NY * NX - 1) * PIECE)]
            remote(rest, rest, s.to_chan, 0, me.partner).wait()
            for quarter in range(4):
                columns = slice(quarter * STRIP, (quarter + 1) * STRIP)
                out_ref[:, columns] = s.final_image[pl.ds(quarter, 2 * NY * NX, stride=4)]
            waits.append(finish)
        else:
            t = of_iteration(s, it + 1)
            t.sky[me.owner * PLANE + me.spot] = estimate.astype(jnp.bfloat16)
            all_sky = spread_sky_plane(me, t.sky, t.to_sky_plane, None)
            s.estimate[...] = estimate
            finish()
            spread_x, spread_pair = sky_spreaders(me, t)
            all_sky.wait_recv()
            for dx in (2, 1, 3):
                spread_x(dx).start()
            spread_pair(0).start()
            for dx in (1, 3, 2):
                spread_x(dx).wait_recv()
                spread_pair(NX - dx).start()
            for dx in range(NX):
                spread_pair(dx).wait()
            for dx in range(1, NX):
                spread_x(dx).wait_send()
            all_sky.wait_send()
    for finish in waits:
        finish()


def on_device(start_image, visibilities, strip_index, live_counts, uv_kernels):
    slot_count = lax.axis_size("chan") * lax.axis_size("facet")
    channels, uvtiles = visibilities.shape[1:3]
    step_size = OWNERS * PIECE / (2.5 * slot_count * channels * uvtiles)
    strips = strip_index.transpose(0, 2, 3, 1).reshape(uvtiles * TERMS, channels)
    counts = live_counts.transpose(0, 2, 1).reshape(uvtiles, channels)
    shapes = scratch_shapes()

    def body(*refs):
        reconstruct_kernel(step_size, list(shapes), *refs)

    return pl.pallas_call(
        body,
        out_shape=jax.ShapeDtypeStruct(start_image.shape, jnp.float32),
        in_specs=[pl.BlockSpec(memory_space=pltpu.VMEM)] * 5,
        out_specs=pl.BlockSpec(memory_space=pltpu.VMEM),
        scratch_shapes=list(shapes.values()),
        compiler_params=pltpu.CompilerParams(collective_id=0, has_side_effects=True),
        name="reconstruct",
    )(start_image, strips, counts, visibilities[0], uv_kernels)


def solution(mesh):
    placed = (
        P(None, "facet"),
        P(("chan", "facet"), None, None, None),
        P(("chan", "facet"), None, None, None),
        P(("chan", "facet"), None, None),
        P("chan", "facet", None, None),
    )
    return jax.shard_map(
        on_device, mesh=mesh, in_specs=placed, out_specs=P(None, "facet"), check_vma=False
    )
```

time: 773 us -> 105 us (0.14)
  waiting for transfers between devices: 650 us -> 0 us
  Pallas kernels: 0 us -> 103 us
  starting transfers between devices: 37.6 us -> 0 us
  other arithmetic: 30 us -> 0 us
  local copies, waits for them, and re-layouts: 31.1 us -> 1.57 us
  between operations: 13.4 us -> 0.01 us
  blocking collectives: 9.83 us -> 0 us
    psum x2 -> x0, waiting for transfers between devices: 555 us -> none  [on_device(): summed = lax.psum(gradient, ('chan', 'facet'))]
    pallas_call x0 -> x1, Pallas kernels: none -> 103 us  [on_device(): pl.pallas_call(body, out_shape=jax.ShapeDtypeStruct(start_image.shape, jn...]
    all_gather x2 -> x0, waiting for transfers between devices: 58.4 us -> none  [on_device(): lax.all_gather(estimate.astype(jnp.bfloat16), 'facet', axis=1, tiled=True)]
    all_to_all x5 -> x0, starting transfers between devices: 37.3 us -> none  [the longest x1 13.6 us: on_device(): lax.all_to_all(lax.all_to_all(live_counts, 'chan', split_axis=1, concat_a...]
    all_to_all x5 -> x0, waiting for transfers between devices: 36.2 us -> none  [the longest x1 13.6 us: on_device(): lax.all_to_all(visibilities, 'chan', split_axis=1, concat_axis=0, tiled=T...]
    scatter-add x2 -> x0, other arithmetic: 24.4 us -> none  [on_device(): gradient = jnp.zeros((strip_count, STRIP), jnp.float32).at[flat_ids].add(...]
    gather x2 -> x0, local copies, waits for them, and re-layouts: 12.4 us -> none  [on_device(): sky_strips[picked_ids]]
    all_to_all x1 -> x0, blocking collectives: 9.83 us -> none  [on_device(): lax.all_to_all(lax.all_to_all(strip_index, 'chan', split_axis=1, concat_a...]
  transfers between devices with their start and end apart: 9 -> 0, of which waited for: 8 -> 0; matrix products, arithmetic and copies ran while one was open for 2% -> 0% of each run, Pallas kernels for 0% -> 0%
where the time goes in v6:
time: 105 us
  Pallas kernels  103 us (98%)
  local copies, waits for them, and re-layouts  1.57 us (1%)
    pallas_call x1, Pallas kernels, on_device(): pl.pallas_call(body, out_shape=jax.ShapeDtypeStruct(start_image.shape, jn...  103 us

profile of v6, /device:TPU:1, one launch (start us, length us, event | category | flops | bytes accessed | tf_op | source)
XLA Modules:
  0.0 104.6 jit_solution(4186623463075156521)
XLA Ops:
  0.0 103.0 %reconstruct.1 = f32[64,512]{1,0:T(8,128)} custom-call(f32[64,512]{1,0:T(8,128)} %refs_0_.1, s32[32,64]{1,0:T(8,128)} %bitcast.8, s32[16,64]{1,0:T(8,128)} %bitcast.9, bf16[64,16,256]{2,1,0:T(8,128)(2,1)} %bitcast.7, bf16[2,1,256,256]{3,2,1,0:T(8,128)(2,1)} %refs_4_.1), custom_call_target="tpu_custom_call" | custom-call | tf_op jit(solution)/shard_map/reconstruct/pallas_call | solution.py:521
  103.0 1.6 %copy.7 = f32[64,512]{1,0:T(8,128)} copy(f32[64,512]{1,0:T(8,128)} %reconstruct.1) | data formatting | bytes 262144

commit v7 on v6

--- a/solution.py
+++ b/solution.py
@@ -71,6 +71,19 @@
     ((dy, dx) for dy in range(NY) for dx in range(NX) if dy or dx),
     key=lambda step: -reach(step[0], NY) - reach(step[1], NX),
 )
+
+
+ROWS_NEAR = sorted(range(NY), key=lambda d: reach(d, NY))
+ROWS_FAR = ROWS_NEAR[::-1]
+COLUMNS_FAR = sorted(range(NZ), key=lambda d: -reach(d, NZ))
+BLOCK_STEPS = ((2, 0), (1, 0), (2, 1), (3, 0), (1, 1), (3, 1), (0, 0), (0, 1))
+
+
+def pick(step, values):
+    value = values[0]
+    for at, other in enumerate(values[1:], 1):
+        value = jnp.where(step == at, other, value)
+    return value
 
 
 def remote(src, dst, sems, at, target):
@@ -184,8 +197,8 @@
         shapes.update(
             {
                 f"sky{it}": vmem((OWNERS, PIECE, STRIP), low),
-                f"to_sky_plane{it}": dma((2, 1)),
-                f"to_sky_x{it}": dma((2, NX)),
+                f"to_sky_plane{it}": dma((2, NY)),
+                f"to_sky_x{it}": dma((2, NX * NY)),
                 f"to_sky_pair{it}": dma((2, NX)),
                 f"got_pair{it}": vmem(blocks, low),
                 f"sum_pair{it}": vmem(blocks, low),
@@ -193,7 +206,7 @@
                 f"sum_x{it}": vmem(blocks[1:], low),
                 f"got_plane{it}": vmem(blocks[1:], low),
                 f"to_pair{it}": dma((2, NX)),
-                f"to_x{it}": dma((2, NX)),
+                f"to_x{it}": dma((2, NX * NY)),
                 f"to_plane{it}": dma((2, 1)),
             }
         )
@@ -232,25 +245,57 @@
                     s.vis_send[owner] = s.mixed[row : row + 4].astype(jnp.bfloat16)
 
 
-def spread_sky_plane(me, sky, sems, source):
-    own = sky.at[me.owner * PLANE + me.spot]
-    for dy, dz in FAR_FIRST:
-        remote(own if source is None else source, own, sems, 0, me.on_plane(dy, dz)[1]).start()
-    others = sky.at[pl.ds(0, PLANE - 1)]
-    return remote(others, others, sems, 0, me.partner)
-
-
-def sky_spreaders(me, t):
-    def own_block(dx):
-        return t.sky.at[pl.ds((me.core * NX + me.xs[dx]) * PLANE, PLANE)]
-
-    def spread_x(dx):
-        return remote(own_block(0), own_block(0), t.to_sky_x, dx, me.on_x(dx))
-
-    def spread_pair(dx):
-        return remote(own_block(dx), own_block(dx), t.to_sky_pair, dx, me.partner)
-
-    return spread_x, spread_pair
+class SkySpread:
+    def __init__(self, me, t, source=None):
+        self.me, self.t = me, t
+        own = t.sky.at[me.owner * PLANE + me.spot]
+        for dy, dz in FAR_FIRST:
+            remote(own if source is None else source, own, t.to_sky_plane, dy, me.on_plane(dy, dz)[1]).start()
+
+    def row(self, dx, dy):
+        me = self.me
+        return self.t.sky.at[pl.ds(((me.core * NX + me.xs[dx]) * NY + me.ys[-dy % NY]) * NZ, NZ)]
+
+    def plane(self, dy):
+        rows = self.t.sky.at[pl.ds(self.me.owner * PLANE, NZ - 1)] if dy == 0 else self.row(0, dy)
+        return remote(rows, rows, self.t.to_sky_plane, dy, self.me.partner)
+
+    def across(self, dx, dy):
+        row = self.row(0, dy)
+        return remote(row, row, self.t.to_sky_x, dx * NY + dy, self.me.on_x(dx))
+
+    def pair(self, dx, dy):
+        row = self.row(dx, dy)
+        return remote(row, row, self.t.to_sky_pair, dx, self.me.partner)
+
+    def whole_pair(self, dx):
+        block = self.t.sky.at[pl.ds((self.me.core * NX + self.me.xs[dx]) * PLANE, PLANE)]
+        return remote(block, block, self.t.to_sky_pair, dx, self.me.partner)
+
+    def pass_rows(self):
+        for dy in ROWS_NEAR:
+            self.plane(dy).wait_recv()
+            for dx in (2, 1, 3):
+                self.across(dx, dy).start()
+            self.pair(0, dy).start()
+
+    def pass_blocks(self):
+        for dy in ROWS_NEAR:
+            for dx in (1, 3, 2):
+                self.across(dx, dy).wait_recv()
+                self.pair(NX - dx, dy).start()
+
+    def arrived(self):
+        for dx in range(NX):
+            self.whole_pair(dx).wait_recv()
+
+    def finish(self):
+        for dy in range(NY):
+            self.plane(dy).wait_send()
+            for dx in range(1, NX):
+                self.across(dx, dy).wait_send()
+        for dx in range(NX):
+            self.whole_pair(dx).wait_send()
 
 
 def pack_numbers(me, s):
@@ -287,8 +332,7 @@
         s.vis_send.at[pl.ds(me.owner * PLANE, PLANE)], s.vis_near.at[pl.ds(0, PLANE)], s.local.at[0]
     )
     own_vis.start()
-    all_sky = spread_sky_plane(me, t.sky, t.to_sky_plane, s.start)
-    spread_x, spread_pair = sky_spreaders(me, t)
+    spread = SkySpread(me, t, s.start)
 
     def near_meta(i):
         return remote(s.numbers, s.near_numbers.at[i], s.to_meta_near, i, me.near(i)[1])
@@ -320,10 +364,7 @@
         remote(s.packed.at[spot], s.index_in.at[dy * NZ + dz], s.to_meta_plane, 0, target).start()
     near_vis(1).wait_recv()
     forward(1)
-    all_sky.wait_recv()
-    for dx in (2, 1, 3):
-        spread_x(dx).start()
-    spread_pair(0).start()
+    spread.pass_rows()
 
     @pl.loop(2, NEAR)
     def _(i):
@@ -337,12 +378,9 @@
     to_smem = pltpu.make_async_copy(s.index_now, s.index_smem, s.local.at[1])
     to_smem.start()
     selectors(s.index_now, s.high_rows, s.low_hits)
-    for dx in (1, 3, 2):
-        spread_x(dx).wait_recv()
-        spread_pair(NX - dx).start()
+    spread.pass_blocks()
     to_smem.wait()
-    for dx in range(NX):
-        spread_pair(dx).wait_recv()
+    spread.arrived()
     gather_rows(s.index_smem, t.sky, s.strips, s.picked)
 
     arrived = s.vis_in.at[pl.ds(1, PLANE - 1)]
@@ -357,11 +395,7 @@
     def finish():
         all_index.wait_send()
         all_vis.wait_send()
-        all_sky.wait_send()
-        for dx in range(1, NX):
-            spread_x(dx).wait_send()
-        for dx in range(NX):
-            spread_pair(dx).wait_send()
+        spread.finish()
         for i in range(1, NEAR):
             near_meta(i).wait_send()
             near_vis(i).wait_send()
@@ -399,46 +433,46 @@
         block = s.image.at[pl.ds(((1 - me.core) * NX + lax.rem(me.x + dx, NX)) * PLANE, PLANE)]
         return remote(block, t.got_pair.at[dx], t.to_pair, dx, me.partner)
 
-    def x_copy(dx):
+    def x_copy(dx, dy):
         target = (me.y * NX + lax.rem(me.x + dx, NX), me.facet)
-        return remote(t.sum_pair.at[dx], t.got_x.at[dx], t.to_x, dx, target)
+        row = pl.ds(me.ys[dy] * NZ, NZ)
+        return remote(t.sum_pair.at[dx, row], t.got_x.at[dx, row], t.to_x, dx * NY + dy, target)
 
     @pl.loop(0, 2 * NX)
     def _(step):
-        dx = lax.rem(step + 1, NX)
-        core = jnp.where(step < NX, 1 - me.core, me.core)
+        dx = pick(step, [shift for shift, _ in BLOCK_STEPS])
+        own = pick(step, [mine for _, mine in BLOCK_STEPS])
+        core = lax.rem(me.core + 1 + own, 2)
         block = core * NX + lax.rem(me.x + dx, NX)
         part = scatter_block(block, s.high_rows, s.low_hits, s.hits, s.adjoint_low)
         s.image[pl.ds(block * PLANE, PLANE)] = part.reshape(PLANE, PIECE, STRIP).astype(jnp.bfloat16)
 
-        @pl.when(step < NX)
+        @pl.when(own == 0)
         def _():
             pair_copy(dx).start()
 
-        @pl.when(jnp.logical_and(step >= NX, step < 2 * NX - 1))
+        @pl.when(jnp.logical_and(own == 1, dx > 0))
         def _():
             pair_copy(dx).wait_recv()
-            for i in range(PLANE // 8):
-                mine = s.image[pl.ds(block * PLANE + i * 8, 8)].astype(jnp.float32)
-                total = mine + t.got_pair[dx, pl.ds(i * 8, 8)].astype(jnp.float32)
-                t.sum_pair[dx, pl.ds(i * 8, 8)] = total.astype(jnp.bfloat16)
-            x_copy(dx).start()
+            for dy in ROWS_FAR:
+                row = pl.ds(me.ys[dy] * NZ, NZ)
+                mine = s.image[pl.ds(block * PLANE + me.ys[dy] * NZ, NZ)].astype(jnp.float32)
+                t.sum_pair[dx, row] = (mine + t.got_pair[dx, row].astype(jnp.float32)).astype(jnp.bfloat16)
+                x_copy(dx, dy).start()
 
     pair_copy(0).wait_recv()
-    for dx in range(1, NX):
-        x_copy(dx).wait_recv()
-
-    @pl.loop(0, PLANE // 8)
-    def _(i):
-        rows = pl.ds(i * 8, 8)
-        total = s.image[pl.ds(me.owner * PLANE + i * 8, 8)].astype(jnp.float32) + t.got_pair[0, rows].astype(jnp.float32)
-        for dx in range(1, NX):
-            total += t.got_x[dx, rows].astype(jnp.float32)
-        t.sum_x[rows] = total.astype(jnp.bfloat16)
-
-    for dy, dz in FAR_FIRST:
-        place, target = me.on_plane(dy, dz)
-        remote(t.sum_x.at[place], t.got_plane.at[dy * NZ + dz], t.to_plane, 0, target).start()
+    for dy in ROWS_FAR:
+        row = pl.ds(me.ys[dy] * NZ, NZ)
+        total = s.image[pl.ds(me.owner * PLANE + me.ys[dy] * NZ, NZ)].astype(jnp.float32)
+        total += t.got_pair[0, row].astype(jnp.float32)
+        for dx in (2, 1, 3):
+            x_copy(dx, dy).wait_recv()
+            total += t.got_x[dx, row].astype(jnp.float32)
+        t.sum_x[row] = total.astype(jnp.bfloat16)
+        for dz in COLUMNS_FAR:
+            if dy or dz:
+                place, target = me.on_plane(dy, dz)
+                remote(t.sum_x.at[place], t.got_plane.at[dy * NZ + dz], t.to_plane, 0, target).start()
     others = t.got_plane.at[pl.ds(1, PLANE - 1)]
     all_plane = remote(others, others, t.to_plane, 0, me.partner)
     all_plane.wait_recv()
@@ -450,7 +484,8 @@
         for dx in range(NX):
             pair_copy(dx).wait_send()
         for dx in range(1, NX):
-            x_copy(dx).wait_send()
+            for dy in range(NY):
+                x_copy(dx, dy).wait_send()
         all_plane.wait_send()
 
     return (parts[0] + parts[1]) + (parts[2] + parts[3]), finish
@@ -487,22 +522,13 @@
         else:
             t = of_iteration(s, it + 1)
             t.sky[me.owner * PLANE + me.spot] = estimate.astype(jnp.bfloat16)
-            all_sky = spread_sky_plane(me, t.sky, t.to_sky_plane, None)
+            spread = SkySpread(me, t)
             s.estimate[...] = estimate
             finish()
-            spread_x, spread_pair = sky_spreaders(me, t)
-            all_sky.wait_recv()
-            for dx in (2, 1, 3):
-                spread_x(dx).start()
-            spread_pair(0).start()
-            for dx in (1, 3, 2):
-                spread_x(dx).wait_recv()
-                spread_pair(NX - dx).start()
-            for dx in range(NX):
-                spread_pair(dx).wait()
-            for dx in range(1, NX):
-                spread_x(dx).wait_send()
-            all_sky.wait_send()
+            spread.pass_rows()
+            spread.pass_blocks()
+            spread.arrived()
+            waits.append(spread.finish)
     for finish in waits:
         finish()
 

time: 105 us -> 100 us (0.952)
  Pallas kernels: 103 us -> 98.2 us
    pallas_call x1, Pallas kernels: 103 us -> 98.2 us  [on_device(): pl.pallas_call(body, out_shape=jax.ShapeDtypeStruct(start_image.shape, jn...]
where the time goes in v7:
time: 100 us; the launch traced here: 99.8 us
  Pallas kernels  98.2 us (98%)
  local copies, waits for them, and re-layouts  1.57 us (2%)
    pallas_call x1, Pallas kernels, on_device(): pl.pallas_call(body, out_shape=jax.ShapeDtypeStruct(start_image.shape, jn...  98.2 us

profile of v7, /device:TPU:1, one launch (start us, length us, event | category | flops | bytes accessed | tf_op | source)
XLA Modules:
  0.0 99.8 jit_solution(9826635415396848588)
XLA Ops:
  0.0 98.2 %reconstruct.1 = f32[64,512]{1,0:T(8,128)} custom-call(f32[64,512]{1,0:T(8,128)} %refs_0_.1, s32[32,64]{1,0:T(8,128)} %bitcast.8, s32[16,64]{1,0:T(8,128)} %bitcast.9, bf16[64,16,256]{2,1,0:T(8,128)(2,1)} %bitcast.7, bf16[2,1,256,256]{3,2,1,0:T(8,128)(2,1)} %refs_4_.1), custom_call_target="tpu_custom_call" | custom-call | tf_op jit(solution)/shard_map/reconstruct/pallas_call | solution.py:547
  98.3 1.6 %copy.7 = f32[64,512]{1,0:T(8,128)} copy(f32[64,512]{1,0:T(8,128)} %reconstruct.1) | data formatting | bytes 262144

commit v8 on v7

--- a/solution.py
+++ b/solution.py
@@ -157,7 +157,7 @@
             setattr(self, name, ref)
 
 
-def scratch_shapes():
+def scratch_shapes(vis_shape, kernel_shape):
     vmem = pltpu.VMEM
     dma = pltpu.SemaphoreType.DMA
     low, wide, whole = jnp.bfloat16, jnp.float32, jnp.int32
@@ -191,7 +191,10 @@
         to_meta_plane=dma((2, 1)),
         to_vis_near=dma((2, NEAR)),
         to_vis_plane=dma((2, 1)),
-        local=dma((2,)),
+        local=dma((5,)),
+        vis_own=vmem(vis_shape, low),
+        weights=vmem(kernel_shape, low),
+        start_rows=vmem((8, 4 * STRIP), wide),
     )
     for it in range(ITERS):
         shapes.update(
@@ -218,10 +221,10 @@
     return Named(names, [getattr(s, name + str(it)) for name in names])
 
 
-def prepare(me, s, start_ref, index_ref, counts_ref, vis_ref):
+def prepare(me, s, index_ref, counts_ref):
     for quarter in range(4):
         columns = slice(quarter * STRIP, (quarter + 1) * STRIP)
-        s.mixed[:8] = start_ref[pl.ds(pl.multiple_of(me.chan // 4 * 8, 8), 8), columns]
+        s.mixed[:8] = s.start_rows[:, columns]
         for low in range(2):
             s.estimate[4 * low + quarter : 4 * low + quarter + 1] = s.mixed[pl.ds(me.chan % 4 * 2 + low, 1)]
     s.start[...] = s.estimate[...].astype(jnp.bfloat16)
@@ -236,7 +239,7 @@
                 chan = (y * NX + x) * 2 + ch
                 live = lane < counts_ref[:, chan : chan + 1]
                 for half in range(2):
-                    block = vis_ref[chan, :, half * STRIP : (half + 1) * STRIP].astype(jnp.float32)
+                    block = s.vis_own[chan, :, half * STRIP : (half + 1) * STRIP].astype(jnp.float32)
                     s.mixed[pl.ds(ch * 2 + half, 2 * NZ, stride=4)] = jnp.where(live, block, FLAGGED)
             for z in range(NZ):
                 for core in range(2):
@@ -332,7 +335,6 @@
         s.vis_send.at[pl.ds(me.owner * PLANE, PLANE)], s.vis_near.at[pl.ds(0, PLANE)], s.local.at[0]
     )
     own_vis.start()
-    spread = SkySpread(me, t, s.start)
 
     def near_meta(i):
         return remote(s.numbers, s.near_numbers.at[i], s.to_meta_near, i, me.near(i)[1])
@@ -346,6 +348,7 @@
         near_meta(i).start()
     for i in range(1, NEAR):
         near_vis(i).start()
+    spread = SkySpread(me, t, s.start)
     own_vis.wait()
 
     def forward(i):
@@ -362,11 +365,14 @@
     for dy, dz in FAR_FIRST:
         spot, target = me.on_plane(dy, dz)
         remote(s.packed.at[spot], s.index_in.at[dy * NZ + dz], s.to_meta_plane, 0, target).start()
-    near_vis(1).wait_recv()
-    forward(1)
+    @pl.loop(1, 6)
+    def _(i):
+        near_vis(i).wait_recv()
+        forward(i)
+
     spread.pass_rows()
 
-    @pl.loop(2, NEAR)
+    @pl.loop(6, NEAR)
     def _(i):
         near_vis(i).wait_recv()
         forward(i)
@@ -494,18 +500,31 @@
 def reconstruct_kernel(step_size, names, start_ref, index_ref, counts_ref, vis_ref, kernel_ref, out_ref, *scratch):
     s = Named(names, scratch)
     me = Place()
+    rows = pl.ds(pl.multiple_of(me.chan // 4 * 8, 8), 8)
+    loads = [
+        pltpu.make_async_copy(source, target, s.local.at[2 + at])
+        for at, (source, target) in enumerate(
+            ((start_ref.at[rows], s.start_rows), (vis_ref, s.vis_own), (kernel_ref, s.weights))
+        )
+    ]
+    for load in loads:
+        load.start()
     wait_for_all = greet(
         [me.on_plane(dy, dz)[1] for dy, dz in FAR_FIRST]
         + [me.on_chan(dy, dx) for dy, dx in CHAN_FAR_FIRST if dy and dx]
         + [me.near(i)[1] for i in range(1, NEAR)]
     )
-    prepare(me, s, start_ref, index_ref, counts_ref, vis_ref)
+    for load in loads[:2]:
+        load.wait()
+    prepare(me, s, index_ref, counts_ref)
     wait_for_all()
     waits = [exchange(me, s)]
     for it in range(ITERS):
         if it:
             gather_rows(s.index_smem, getattr(s, f"sky{it}"), s.strips, s.picked)
-        back_projected(s, kernel_ref)
+        else:
+            loads[2].wait()
+        back_projected(s, s.weights)
         gradient, finish = reduce_gradient(me, s, it)
         estimate = jnp.maximum(s.estimate[...] - step_size * gradient - shrinkage, 0.0)
         if it == ITERS - 1:
@@ -539,7 +558,7 @@
     step_size = OWNERS * PIECE / (2.5 * slot_count * channels * uvtiles)
     strips = strip_index.transpose(0, 2, 3, 1).reshape(uvtiles * TERMS, channels)
     counts = live_counts.transpose(0, 2, 1).reshape(uvtiles, channels)
-    shapes = scratch_shapes()
+    shapes = scratch_shapes(visibilities.shape[1:], uv_kernels.shape)
 
     def body(*refs):
         reconstruct_kernel(step_size, list(shapes), *refs)
@@ -547,7 +566,7 @@
     return pl.pallas_call(
         body,
         out_shape=jax.ShapeDtypeStruct(start_image.shape, jnp.float32),
-        in_specs=[pl.BlockSpec(memory_space=pltpu.VMEM)] * 5,
+        in_specs=[pl.BlockSpec(memory_space=space) for space in (pl.ANY, pltpu.VMEM, pltpu.VMEM, pl.ANY, pl.ANY)],
         out_specs=pl.BlockSpec(memory_space=pltpu.VMEM),
         scratch_shapes=list(shapes.values()),
         compiler_params=pltpu.CompilerParams(collective_id=0, has_side_effects=True),

time: 100 us -> 99.4 us (level)
  no operation moved by 1% of the time
where the time goes in v8:
time: 99.4 us; the launch traced here: 99.1 us
  Pallas kernels  97.5 us (98%)
  local copies, waits for them, and re-layouts  1.57 us (2%)
    pallas_call x1, Pallas kernels, on_device(): pl.pallas_call(body, out_shape=jax.ShapeDtypeStruct(start_image.shape, jn...  97.5 us

profile of v8, /device:TPU:1, one launch (start us, length us, event | category | flops | bytes accessed | tf_op | source)
XLA Modules:
  0.0 99.1 jit_solution(3931561663074922983)
XLA Ops:
  0.0 97.5 %reconstruct.1 = f32[64,512]{1,0:T(8,128)} custom-call(f32[64,512]{1,0:T(8,128)} %refs_0_.1, s32[32,64]{1,0:T(8,128)} %bitcast.8, s32[16,64]{1,0:T(8,128)} %bitcast.9, bf16[64,16,256]{2,1,0:T(8,128)(2,1)} %bitcast.7, bf16[2,1,256,256]{3,2,1,0:T(8,128)(2,1)} %refs_4_.1), custom_call_target="tpu_custom_call" | custom-call | tf_op jit(solution)/shard_map/reconstruct/pallas_call | solution.py:566
  97.5 1.6 %copy.7 = f32[64,512]{1,0:T(8,128)} copy(f32[64,512]{1,0:T(8,128)} %reconstruct.1) | data formatting | bytes 262144

commit v9 on v8

--- a/solution.py
+++ b/solution.py
@@ -114,12 +114,14 @@
     return (((core * NX + x) * NY + y) * NZ + z) * PIECE + low_row * 4 + quarter
 
 
-def gather_rows(index_smem, sky_ref, strips, picked):
-    @pl.loop(0, OWNERS // 8)
+def widen(core, sky_ref, strips):
+    @pl.loop(core * (OWNERS // 16), (core + 1) * (OWNERS // 16))
     def _(i):
         block = sky_ref[pl.ds(i * 8, 8)].astype(jnp.float32)
         strips[pl.ds(pl.multiple_of(i * 64, 64), 64)] = block.reshape(64, STRIP)
 
+
+def gather_rows(index_smem, strips, picked):
     @pl.loop(0, PLANE)
     def _(k):
         for i in range(NEAR):
@@ -386,8 +388,10 @@
     selectors(s.index_now, s.high_rows, s.low_hits)
     spread.pass_blocks()
     to_smem.wait()
+    widen(me.core, t.sky, s.strips)
     spread.arrived()
-    gather_rows(s.index_smem, t.sky, s.strips, s.picked)
+    widen(1 - me.core, t.sky, s.strips)
+    gather_rows(s.index_smem, s.strips, s.picked)
 
     arrived = s.vis_in.at[pl.ds(1, PLANE - 1)]
     all_vis = remote(arrived, arrived, s.to_vis_plane, 0, me.partner)
@@ -521,7 +525,7 @@
     waits = [exchange(me, s)]
     for it in range(ITERS):
         if it:
-            gather_rows(s.index_smem, getattr(s, f"sky{it}"), s.strips, s.picked)
+            gather_rows(s.index_smem, s.strips, s.picked)
         else:
             loads[2].wait()
         back_projected(s, s.weights)
@@ -546,7 +550,9 @@
             finish()
             spread.pass_rows()
             spread.pass_blocks()
+            widen(me.core, t.sky, s.strips)
             spread.arrived()
+            widen(1 - me.core, t.sky, s.strips)
             waits.append(spread.finish)
     for finish in waits:
         finish()

time: 99.4 us -> 99.3 us (level)
  no operation moved by 1% of the time
where the time goes in v9:
time: 99.3 us; the launch traced here: 99 us
  Pallas kernels  97.4 us (98%)
  local copies, waits for them, and re-layouts  1.57 us (2%)
    pallas_call x1, Pallas kernels, on_device(): pl.pallas_call(body, out_shape=jax.ShapeDtypeStruct(start_image.shape, jn...  97.4 us

profile of v9, /device:TPU:1, one launch (start us, length us, event | category | flops | bytes accessed | tf_op | source)
XLA Modules:
  0.0 99.0 jit_solution(12619446094932520293)
XLA Ops:
  0.0 97.4 %reconstruct.1 = f32[64,512]{1,0:T(8,128)} custom-call(f32[64,512]{1,0:T(8,128)} %refs_0_.1, s32[32,64]{1,0:T(8,128)} %bitcast.8, s32[16,64]{1,0:T(8,128)} %bitcast.9, bf16[64,16,256]{2,1,0:T(8,128)(2,1)} %bitcast.7, bf16[2,1,256,256]{3,2,1,0:T(8,128)(2,1)} %refs_4_.1), custom_call_target="tpu_custom_call" | custom-call | tf_op jit(solution)/shard_map/reconstruct/pallas_call | solution.py:572
  97.4 1.6 %copy.7 = f32[64,512]{1,0:T(8,128)} copy(f32[64,512]{1,0:T(8,128)} %reconstruct.1) | data formatting | bytes 262144
